TPU v7x, 128 devices: a whole 4x4x4 slice. The times are simulated.
128 devices in a mesh: elem: 32 (over x, z, core), band: 4 (over y).
Axes of the slice: x: 4, y: 4, z: 4, core: 2. Of those that a mesh axis runs over, the one named last changes fastest.
Arguments:
- crm_state: bfloat16 [32, 128, 6, 3840], P('elem', 'band'), may hold values from -6 to 6
- host_state: float32 [72, 32, 128], P(None, 'elem', 'band'), may hold values from -6 to 6
- kappa: float32 [32, 128], P('elem', 'band'), may hold values from 0.02 to 0.2
- substeps: int32 [32, 128], P('elem', 'band'), may hold values from 1 to 4, as said below
- coupling: float32 [6, 6], replicated, may hold values from -2.5 to 2.5
- level_map: float32 [60, 72], replicated, may hold values from -0.75 to 0.75
- field_scale: float32 [6], replicated, may hold values from 0.5 to 1.5
- back_map: float32 [72, 60], replicated, may hold values from -0.75 to 0.75
- back_weight: float32 [6], replicated, may hold values from -3 to 3
Outputs:
- crm_final: bfloat16 [32, 128, 6, 3840], P('elem', 'band')
- host_final: float32 [72, 32, 128], P(None, 'elem', 'band')
Inputs may be any that keep to these rules, and one draw needn't show every extreme that they name: Each aligned block of 1 x 32 columns (the columns of one device) draws a level from 1 to 4; each column of the block takes 1 plus a uniform integer modulo that level substeps. Column (0, 0) takes 4 substeps and column (0, 1) takes 1.
All inputs are finite; a program needn't handle non-finite values.
Results may differ from a plain program's by a relative error of at most 0.0055.
Values may be sent and summed in bfloat16 or wider, within the bound.
A program may use at most 128 MiB of HBM per device.

v0:
```python
import jax
import jax.numpy as jnp
from jax import lax
from jax.sharding import PartitionSpec as P

FIELDS = 6
NZC = 60
NXC = 64
SUB = 4
WINDOWS = 2


cloud_step = 0.1
return_scale = 1.0


def extended_2(block, sides, width):
    for axis, dim in sides:
        count = lax.axis_size(axis)
        forward = [(i, i + 1) for i in range(count - 1)]
        forward.append((count - 1, 0))
        backward = [(target, source) for source, target in forward]
        low = lax.ppermute(
            lax.slice_in_dim(block, block.shape[dim] - width, None, axis=dim), axis, forward
        )
        high = lax.ppermute(lax.slice_in_dim(block, 0, width, axis=dim), axis, backward)
        block = jnp.concatenate([low, block, high], axis=dim)
    return block


def cloud_substep(fields, forcing_cells, coupling, active, xplace):
    highest = lax.Precision.HIGHEST
    cells = fields.shape[-1]
    zero_rows = jnp.zeros(fields.shape[:-1] + (NXC,), jnp.float32)
    extended = jnp.concatenate([zero_rows, fields, zero_rows], -1)
    next_main = extended[..., NXC + 1 : NXC + 1 + cells]
    next_wrap = extended[..., 1 : 1 + cells]
    prev_main = extended[..., NXC - 1 : NXC - 1 + cells]
    prev_wrap = extended[..., 2 * NXC - 1 : 2 * NXC - 1 + cells]
    plus = jnp.where(xplace == NXC - 1, next_wrap, next_main)
    minus = jnp.where(xplace == 0, prev_wrap, prev_main)
    upper = extended[..., 2 * NXC : 2 * NXC + cells]
    lower = extended[..., 0:cells]
    deriv = 0.5 * (plus - minus)
    vertical = upper - 2.0 * fields + lower
    mixing = jnp.tanh(jnp.einsum("fg,bgp->bfp", coupling, fields, precision=highest))
    change = cloud_step * (-fields[:, 0:1] * deriv + vertical + mixing + forcing_cells)
    return fields + jnp.where(active[:, None, None], change, 0.0)


def cloud_run(state, host_cols, counts, coupling, level_map, field_scale, back_map, back_weight):
    highest = lax.Precision.HIGHEST
    slices = state.shape[0]
    nblocks = 8
    block = slices // nblocks
    order = jnp.argsort(-counts, stable=True)
    inverse = jnp.argsort(order, stable=True)
    fields = jnp.take(state, order, axis=0)
    sorted_cols = jnp.take(host_cols, order, axis=0)
    sorted_counts = jnp.take(counts, order, axis=0)
    mapped = jnp.dot(
        sorted_cols, level_map.T, precision=highest, preferred_element_type=jnp.float32
    )
    forcing = field_scale[None, :, None] * mapped[:, None, :]
    forcing_cells = jnp.repeat(forcing, NXC, axis=-1)
    xplace = jnp.arange(fields.shape[-1], dtype=jnp.int32) % NXC
    start = fields
    field_blocks = fields.reshape((nblocks, block) + fields.shape[1:])
    force_blocks = forcing_cells.reshape((nblocks, block) + forcing_cells.shape[1:])
    count_blocks = sorted_counts.reshape(nblocks, block)
    for turn in range(SUB):

        def advance(carry, items, turn=turn):
            piece, force_piece, count_piece = items
            live = count_piece > turn
            moved = lax.cond(
                jnp.any(live),
                lambda p: cloud_substep(p, force_piece, coupling, live, xplace),
                lambda p: p,
                piece,
            )
            return (carry, moved)

        unused, field_blocks = lax.scan(advance, 0, (field_blocks, force_blocks, count_blocks))
    fields = field_blocks.reshape(fields.shape)
    mean = jnp.mean((fields - start).reshape(slices, FIELDS, NZC, NXC), axis=-1)
    mixed = jnp.einsum("f,nfz->nz", back_weight, mean, precision=highest)
    tend = return_scale * jnp.dot(
        mixed, back_map.T, precision=highest, preferred_element_type=jnp.float32
    )
    return (jnp.take(fields, inverse, axis=0), jnp.take(tend, inverse, axis=0))


def host_section(host, tend_cols, kappa):
    levels = host.shape[0]
    tend = tend_cols.T.reshape(host.shape)
    stacked = jnp.concatenate([host, kappa[None]], 0)
    padded = extended_2(stacked, (("elem", 1), ("band", 2)), 1)
    host_pad = padded[:levels]
    kappa_pad = padded[levels]
    centre = host_pad[:, 1:-1, 1:-1]
    kappa_mid = kappa_pad[1:-1, 1:-1]

    def face(host_near, kappa_near):
        return 0.5 * (kappa_mid + kappa_near) * (host_near - centre)

    spread = face(host_pad[:, 2:, 1:-1], kappa_pad[2:, 1:-1]) + face(
        host_pad[:, :-2, 1:-1], kappa_pad[:-2, 1:-1]
    )
    spread = (
        spread
        + face(host_pad[:, 1:-1, 2:], kappa_pad[1:-1, 2:])
        + face(host_pad[:, 1:-1, :-2], kappa_pad[1:-1, :-2])
    )
    return centre + (tend + spread)


def host_columns(host):
    return host.reshape(host.shape[0], -1).T


def body(
    crm_state, host_state, kappa, substeps, coupling, level_map, field_scale, back_map, back_weight
):
    slices = crm_state.shape[0] * crm_state.shape[1]
    state = crm_state.reshape(slices, crm_state.shape[2], crm_state.shape[3]).astype(jnp.float32)
    counts = substeps.reshape(slices)
    count_values = counts.astype(jnp.float32)
    host = host_state
    params = (coupling, level_map, field_scale, back_map, back_weight)
    for window in range(WINDOWS):
        got_state, got_cols, got_values = (
            lax.all_to_all(state, "elem", split_axis=0, concat_axis=0, tiled=True),
            lax.all_to_all(host_columns(host), "elem", split_axis=0, concat_axis=0, tiled=True),
            lax.all_to_all(count_values, "elem", split_axis=0, concat_axis=0, tiled=True),
        )
        moved, tend = cloud_run(got_state, got_cols, got_values.astype(jnp.int32), *params)
        if window < WINDOWS - 1:
            state, tend = (
                lax.all_to_all(moved, "elem", split_axis=0, concat_axis=0, tiled=True),
                lax.all_to_all(tend, "elem", split_axis=0, concat_axis=0, tiled=True),
            )
        else:
            state = lax.all_to_all(
                moved.astype(jnp.bfloat16), "elem", split_axis=0, concat_axis=0, tiled=True
            )
            tend = lax.all_to_all(tend, "elem", split_axis=0, concat_axis=0, tiled=True)
        host = host_section(host, tend, kappa)
    crm_final = state.reshape(crm_state.shape)
    return (crm_final, host)


def solution(mesh):
    return jax.shard_map(
        body,
        mesh=mesh,
        in_specs=(
            P("elem", "band", None, None),
            P(None, "elem", "band"),
            P("elem", "band"),
            P("elem", "band"),
            P(),
            P(),
            P(),
            P(),
            P(),
        ),
        out_specs=(P("elem", "band", None, None), P(None, "elem", "band")),
        check_vma=False,
    )
```

profile of v0, /device:TPU:0, one launch (start us, length us, event | category | flops | bytes accessed | tf_op | source)
XLA Modules:
  0.0 1091.0 jit_solution(10826208724616299748)
XLA Ops:
  1.4 15.4 %all_to_all.75 = f32[32,1,1]{2,1,0:T(1,128)S(1)} all-to-all(f32[32,1,1]{2,1,0:T(1,128)S(1)} %copy.55), channel_id=1, replica_groups=mesh['elem'=32,'band'=4] {'elem'}, dimensions={0} | all-to-all | bytes 256 | tf_op jit(solution)/shard_map/all_to_all | solution.py:135
  43.6 35.6 %collective-permute-done = f32[73,1,32]{0,2,1:T(8,128)S(1)} collective-permute-done((f32[73,1,32]{0,2,1:T(8,128)S(1)}, f32[73,1,32]{0,2,1:T(8,128)S(1)}, u32[]{:S(2)}, u32[]{:S(2)}) %collective-permute-start) | collective-permute-done | bytes 9376 | tf_op jit(solution)/shard_map/ppermute | solution.py:23
  96.4 141.0 %while.96 = (s32[]{:T(128)}, f32[8,4,6,3840]{3,2,1,0:T(8,128)}, s32[8,4]{1,0:T(8,128)S(1)}, f32[8,4,6,3840]{3,2,1,0:T(8,128)}, f32[6,6]{1,0:T(8,128)S(1)}, /*index=5*/f32[32,6,60]{2,0,1:T(8,128)S(1)}, s32[]{:T(128)}, s32[]{:T(128)}) while((s32[]{:T(128)}, f32[8,4,6,3840]{3,2,1,0:T(8,128)}, s32[8,4]{1,0:T(8,128)S(1)}, ...), condition=%wide.region_5.9_spmd.clone.clone, body=%wide.region_1.8_spmd.clone.clone.sunk | while | flops 7895050 | bytes 15622023 | solution.py:84
  99.1 14.3 %conditional.32 = (f32[1,4,6,3840]{3,2,1,0:T(8,128)S(1)}) conditional(s32[]{:T(128)} %convert_element_type.88, f32[4,6,3840]{2,1,0:T(8,128)S(1)} %dynamic-slice_bitcast_fusion.16, (pred[1,4]{1,0:T(4,128)(4,1)S(1)}, s32[3840]{0:T(1024)S(1)}, f32[4,6,3840]{2,1,0:T(8,128)S(1)}, s32[3840]{0:T(1024)S(1)}, f32[6,6]{1,0:T(8,128)S(1)}, ...), branch_computations={%region_3.6_spmd, %region_4.7_spmd.clone} | conditional | flops 7891200 | bytes 13255868 | solution.py:76
  116.7 14.3 %conditional.32 = (f32[1,4,6,3840]{3,2,1,0:T(8,128)S(1)}) conditional(s32[]{:T(128)} %convert_element_type.88, f32[4,6,3840]{2,1,0:T(8,128)S(1)} %dynamic-slice_bitcast_fusion.16, (pred[1,4]{1,0:T(4,128)(4,1)S(1)}, s32[3840]{0:T(1024)S(1)}, f32[4,6,3840]{2,1,0:T(8,128)S(1)}, s32[3840]{0:T(1024)S(1)}, f32[6,6]{1,0:T(8,128)S(1)}, ...), branch_computations={%region_3.6_spmd, %region_4.7_spmd.clone} | conditional | flops 7891200 | bytes 13255868 | solution.py:76
  134.3 14.3 %conditional.32 = (f32[1,4,6,3840]{3,2,1,0:T(8,128)S(1)}) conditional(s32[]{:T(128)} %convert_element_type.88, f32[4,6,3840]{2,1,0:T(8,128)S(1)} %dynamic-slice_bitcast_fusion.16, (pred[1,4]{1,0:T(4,128)(4,1)S(1)}, s32[3840]{0:T(1024)S(1)}, f32[4,6,3840]{2,1,0:T(8,128)S(1)}, s32[3840]{0:T(1024)S(1)}, f32[6,6]{1,0:T(8,128)S(1)}, ...), branch_computations={%region_3.6_spmd, %region_4.7_spmd.clone} | conditional | flops 7891200 | bytes 13255868 | solution.py:76
  151.8 14.3 %conditional.32 = (f32[1,4,6,3840]{3,2,1,0:T(8,128)S(1)}) conditional(s32[]{:T(128)} %convert_element_type.88, f32[4,6,3840]{2,1,0:T(8,128)S(1)} %dynamic-slice_bitcast_fusion.16, (pred[1,4]{1,0:T(4,128)(4,1)S(1)}, s32[3840]{0:T(1024)S(1)}, f32[4,6,3840]{2,1,0:T(8,128)S(1)}, s32[3840]{0:T(1024)S(1)}, f32[6,6]{1,0:T(8,128)S(1)}, ...), branch_computations={%region_3.6_spmd, %region_4.7_spmd.clone} | conditional | flops 7891200 | bytes 13255868 | solution.py:76
  169.4 14.3 %conditional.32 = (f32[1,4,6,3840]{3,2,1,0:T(8,128)S(1)}) conditional(s32[]{:T(128)} %convert_element_type.88, f32[4,6,3840]{2,1,0:T(8,128)S(1)} %dynamic-slice_bitcast_fusion.16, (pred[1,4]{1,0:T(4,128)(4,1)S(1)}, s32[3840]{0:T(1024)S(1)}, f32[4,6,3840]{2,1,0:T(8,128)S(1)}, s32[3840]{0:T(1024)S(1)}, f32[6,6]{1,0:T(8,128)S(1)}, ...), branch_computations={%region_3.6_spmd, %region_4.7_spmd.clone} | conditional | flops 7891200 | bytes 13255868 | solution.py:76
  187.0 14.3 %conditional.32 = (f32[1,4,6,3840]{3,2,1,0:T(8,128)S(1)}) conditional(s32[]{:T(128)} %convert_element_type.88, f32[4,6,3840]{2,1,0:T(8,128)S(1)} %dynamic-slice_bitcast_fusion.16, (pred[1,4]{1,0:T(4,128)(4,1)S(1)}, s32[3840]{0:T(1024)S(1)}, f32[4,6,3840]{2,1,0:T(8,128)S(1)}, s32[3840]{0:T(1024)S(1)}, f32[6,6]{1,0:T(8,128)S(1)}, ...), branch_computations={%region_3.6_spmd, %region_4.7_spmd.clone} | conditional | flops 7891200 | bytes 13255868 | solution.py:76
  204.6 14.3 %conditional.32 = (f32[1,4,6,3840]{3,2,1,0:T(8,128)S(1)}) conditional(s32[]{:T(128)} %convert_element_type.88, f32[4,6,3840]{2,1,0:T(8,128)S(1)} %dynamic-slice_bitcast_fusion.16, (pred[1,4]{1,0:T(4,128)(4,1)S(1)}, s32[3840]{0:T(1024)S(1)}, f32[4,6,3840]{2,1,0:T(8,128)S(1)}, s32[3840]{0:T(1024)S(1)}, f32[6,6]{1,0:T(8,128)S(1)}, ...), branch_computations={%region_3.6_spmd, %region_4.7_spmd.clone} | conditional | flops 7891200 | bytes 13255868 | solution.py:76
  222.2 14.3 %conditional.32 = (f32[1,4,6,3840]{3,2,1,0:T(8,128)S(1)}) conditional(s32[]{:T(128)} %convert_element_type.88, f32[4,6,3840]{2,1,0:T(8,128)S(1)} %dynamic-slice_bitcast_fusion.16, (pred[1,4]{1,0:T(4,128)(4,1)S(1)}, s32[3840]{0:T(1024)S(1)}, f32[4,6,3840]{2,1,0:T(8,128)S(1)}, s32[3840]{0:T(1024)S(1)}, f32[6,6]{1,0:T(8,128)S(1)}, ...), branch_computations={%region_3.6_spmd, %region_4.7_spmd.clone} | conditional | flops 7891200 | bytes 13255868 | solution.py:76
  239.6 83.4 %while.97 = (s32[]{:T(128)}, f32[8,4,6,3840]{3,2,1,0:T(8,128)}, s32[8,4]{1,0:T(8,128)S(1)}, f32[8,4,6,3840]{3,2,1,0:T(8,128)}, f32[6,6]{1,0:T(8,128)S(1)}, /*index=5*/f32[32,6,60]{2,0,1:T(8,128)S(1)}, s32[]{:T(128)}, s32[]{:T(128)}) while((s32[]{:T(128)}, f32[8,4,6,3840]{3,2,1,0:T(8,128)}, s32[8,4]{1,0:T(8,128)S(1)}, ...), condition=%wide.region_10.14_spmd.clone.clone, body=%wide.region_6.13_spmd.clone.clone.sunk | while | flops 7895050 | bytes 15622023 | solution.py:84
  242.0 14.3 %conditional.33 = (f32[1,4,6,3840]{3,2,1,0:T(8,128)S(1)}) conditional(s32[]{:T(128)} %convert_element_type.89, f32[4,6,3840]{2,1,0:T(8,128)S(1)} %dynamic-slice_bitcast_fusion.17, (pred[1,4]{1,0:T(4,128)(4,1)S(1)}, s32[3840]{0:T(1024)S(1)}, f32[4,6,3840]{2,1,0:T(8,128)S(1)}, s32[3840]{0:T(1024)S(1)}, f32[6,6]{1,0:T(8,128)S(1)}, ...), branch_computations={%region_8.11_spmd, %region_9.12_spmd.clone} | conditional | flops 7891200 | bytes 13255868 | solution.py:76
  259.6 14.3 %conditional.33 = (f32[1,4,6,3840]{3,2,1,0:T(8,128)S(1)}) conditional(s32[]{:T(128)} %convert_element_type.89, f32[4,6,3840]{2,1,0:T(8,128)S(1)} %dynamic-slice_bitcast_fusion.17, (pred[1,4]{1,0:T(4,128)(4,1)S(1)}, s32[3840]{0:T(1024)S(1)}, f32[4,6,3840]{2,1,0:T(8,128)S(1)}, s32[3840]{0:T(1024)S(1)}, f32[6,6]{1,0:T(8,128)S(1)}, ...), branch_computations={%region_8.11_spmd, %region_9.12_spmd.clone} | conditional | flops 7891200 | bytes 13255868 | solution.py:76
  277.2 14.3 %conditional.33 = (f32[1,4,6,3840]{3,2,1,0:T(8,128)S(1)}) conditional(s32[]{:T(128)} %convert_element_type.89, f32[4,6,3840]{2,1,0:T(8,128)S(1)} %dynamic-slice_bitcast_fusion.17, (pred[1,4]{1,0:T(4,128)(4,1)S(1)}, s32[3840]{0:T(1024)S(1)}, f32[4,6,3840]{2,1,0:T(8,128)S(1)}, s32[3840]{0:T(1024)S(1)}, f32[6,6]{1,0:T(8,128)S(1)}, ...), branch_computations={%region_8.11_spmd, %region_9.12_spmd.clone} | conditional | flops 7891200 | bytes 13255868 | solution.py:76
  294.8 14.3 %conditional.33 = (f32[1,4,6,3840]{3,2,1,0:T(8,128)S(1)}) conditional(s32[]{:T(128)} %convert_element_type.89, f32[4,6,3840]{2,1,0:T(8,128)S(1)} %dynamic-slice_bitcast_fusion.17, (pred[1,4]{1,0:T(4,128)(4,1)S(1)}, s32[3840]{0:T(1024)S(1)}, f32[4,6,3840]{2,1,0:T(8,128)S(1)}, s32[3840]{0:T(1024)S(1)}, f32[6,6]{1,0:T(8,128)S(1)}, ...), branch_computations={%region_8.11_spmd, %region_9.12_spmd.clone} | conditional | flops 7891200 | bytes 13255868 | solution.py:76
  325.3 69.0 %while.98 = (s32[]{:T(128)}, f32[8,4,6,3840]{3,2,1,0:T(8,128)}, s32[8,4]{1,0:T(8,128)S(1)}, f32[8,4,6,3840]{3,2,1,0:T(8,128)}, f32[6,6]{1,0:T(8,128)S(1)}, /*index=5*/f32[32,6,60]{2,0,1:T(8,128)S(1)}, s32[]{:T(128)}, s32[]{:T(128)}) while((s32[]{:T(128)}, f32[8,4,6,3840]{3,2,1,0:T(8,128)}, s32[8,4]{1,0:T(8,128)S(1)}, ...), condition=%wide.region_15.19_spmd.clone.clone, body=%wide.region_11.18_spmd.clone.clone.sunk | while | flops 7895050 | bytes 15622023 | solution.py:84
  345.3 14.3 %conditional.34 = (f32[1,4,6,3840]{3,2,1,0:T(8,128)S(1)}) conditional(s32[]{:T(128)} %convert_element_type.90, f32[4,6,3840]{2,1,0:T(8,128)S(1)} %dynamic-slice_bitcast_fusion.18, (pred[1,4]{1,0:T(4,128)(4,1)S(1)}, s32[3840]{0:T(1024)S(1)}, f32[4,6,3840]{2,1,0:T(8,128)S(1)}, s32[3840]{0:T(1024)S(1)}, f32[6,6]{1,0:T(8,128)S(1)}, ...), branch_computations={%region_13.16_spmd, %region_14.17_spmd.clone} | conditional | flops 7891200 | bytes 13255868 | solution.py:76
  362.9 14.3 %conditional.34 = (f32[1,4,6,3840]{3,2,1,0:T(8,128)S(1)}) conditional(s32[]{:T(128)} %convert_element_type.90, f32[4,6,3840]{2,1,0:T(8,128)S(1)} %dynamic-slice_bitcast_fusion.18, (pred[1,4]{1,0:T(4,128)(4,1)S(1)}, s32[3840]{0:T(1024)S(1)}, f32[4,6,3840]{2,1,0:T(8,128)S(1)}, s32[3840]{0:T(1024)S(1)}, f32[6,6]{1,0:T(8,128)S(1)}, ...), branch_computations={%region_13.16_spmd, %region_14.17_spmd.clone} | conditional | flops 7891200 | bytes 13255868 | solution.py:76
  396.6 40.9 %while.99 = (s32[]{:T(128)}, f32[8,4,6,3840]{3,2,1,0:T(8,128)}, s32[8,4]{1,0:T(8,128)S(1)}, f32[8,4,6,3840]{3,2,1,0:T(8,128)}, f32[6,6]{1,0:T(8,128)S(1)}, /*index=5*/f32[32,6,60]{2,0,1:T(8,128)S(1)}, s32[]{:T(128)}, s32[]{:T(128)}) while((s32[]{:T(128)}, f32[8,4,6,3840]{3,2,1,0:T(8,128)}, s32[8,4]{1,0:T(8,128)S(1)}, ...), condition=%wide.region_20.24_spmd.clone.clone, body=%wide.region_16.23_spmd.clone.clone.sunk | while | flops 7895050 | bytes 15622023 | solution.py:84
  399.0 14.3 %conditional.35 = (f32[1,4,6,3840]{3,2,1,0:T(8,128)S(1)}) conditional(s32[]{:T(128)} %convert_element_type.91, f32[4,6,3840]{2,1,0:T(8,128)S(1)} %dynamic-slice_bitcast_fusion.19, (pred[1,4]{1,0:T(4,128)(4,1)S(1)}, s32[3840]{0:T(1024)S(1)}, f32[4,6,3840]{2,1,0:T(8,128)S(1)}, s32[3840]{0:T(1024)S(1)}, f32[6,6]{1,0:T(8,128)S(1)}, ...), branch_computations={%region_18.21_spmd, %region_19.22_spmd.clone} | conditional | flops 7891200 | bytes 13255868 | solution.py:76
  453.2 18.4 %all-to-all-start.5 = ((f32[32,1,72]{2,1,0:T(1,128)}), f32[32,1,72]{2,1,0:T(1,128)S(1)}, u32[]{:S(2)}, u32[]{:S(2)}) async-start(f32[32,1,72]{2,1,0:T(1,128)} %bitcast.61), calls=%async_computation.5 | async-start | bytes 32768 | tf_op jit(solution)/shard_map/all_to_all | solution.py:141
  491.9 52.4 %all_to_all.76 = f32[32,6,3840]{2,1,0:T(8,128)} all-to-all(f32[32,6,3840]{2,1,0:T(8,128)} %broadcast_select_fusion.1), channel_id=1, replica_groups=mesh['elem'=32,'band'=4] {'elem'}, dimensions={0} | all-to-all | bytes 5898240 | tf_op jit(solution)/shard_map/all_to_all | solution.py:140
  550.4 48.6 %all-to-all-done.4 = f32[32,6,3840]{2,1,0:T(8,128)} async-done(((f32[32,6,3840]{2,1,0:T(8,128)}), f32[32,6,3840]{2,1,0:T(8,128)}, u32[]{:S(2)}, u32[]{:S(2)}) %all-to-all-start.4) | async-done | bytes 2949152 | tf_op jit(solution)/shard_map/all_to_all | solution.py:133
  610.9 140.8 %while.100 = (s32[]{:T(128)}, f32[8,4,6,3840]{3,2,1,0:T(8,128)}, s32[8,4]{1,0:T(8,128)S(1)}, f32[8,4,6,3840]{3,2,1,0:T(8,128)}, f32[6,6]{1,0:T(8,128)S(1)}, /*index=5*/f32[32,6,60]{2,0,1:T(8,128)S(1)}, s32[]{:T(128)}, s32[]{:T(128)}) while((s32[]{:T(128)}, f32[8,4,6,3840]{3,2,1,0:T(8,128)}, s32[8,4]{1,0:T(8,128)S(1)}, ...), condition=%wide.region_27.31_spmd.clone.clone, body=%wide.region_23.30_spmd.clone.clone.sunk | while | flops 7895050 | bytes 15622023 | solution.py:84
  613.3 14.3 %conditional.36 = (f32[1,4,6,3840]{3,2,1,0:T(8,128)S(1)}) conditional(s32[]{:T(128)} %convert_element_type.92, f32[4,6,3840]{2,1,0:T(8,128)S(1)} %dynamic-slice_bitcast_fusion.20, (pred[1,4]{1,0:T(4,128)(4,1)S(1)}, s32[3840]{0:T(1024)S(1)}, f32[4,6,3840]{2,1,0:T(8,128)S(1)}, s32[3840]{0:T(1024)S(1)}, f32[6,6]{1,0:T(8,128)S(1)}, ...), branch_computations={%region_25.28_spmd, %region_26.29_spmd.clone} | conditional | flops 7891200 | bytes 13255868 | solution.py:76
  630.9 14.3 %conditional.36 = (f32[1,4,6,3840]{3,2,1,0:T(8,128)S(1)}) conditional(s32[]{:T(128)} %convert_element_type.92, f32[4,6,3840]{2,1,0:T(8,128)S(1)} %dynamic-slice_bitcast_fusion.20, (pred[1,4]{1,0:T(4,128)(4,1)S(1)}, s32[3840]{0:T(1024)S(1)}, f32[4,6,3840]{2,1,0:T(8,128)S(1)}, s32[3840]{0:T(1024)S(1)}, f32[6,6]{1,0:T(8,128)S(1)}, ...), branch_computations={%region_25.28_spmd, %region_26.29_spmd.clone} | conditional | flops 7891200 | bytes 13255868 | solution.py:76
  648.5 14.3 %conditional.36 = (f32[1,4,6,3840]{3,2,1,0:T(8,128)S(1)}) conditional(s32[]{:T(128)} %convert_element_type.92, f32[4,6,3840]{2,1,0:T(8,128)S(1)} %dynamic-slice_bitcast_fusion.20, (pred[1,4]{1,0:T(4,128)(4,1)S(1)}, s32[3840]{0:T(1024)S(1)}, f32[4,6,3840]{2,1,0:T(8,128)S(1)}, s32[3840]{0:T(1024)S(1)}, f32[6,6]{1,0:T(8,128)S(1)}, ...), branch_computations={%region_25.28_spmd, %region_26.29_spmd.clone} | conditional | flops 7891200 | bytes 13255868 | solution.py:76
  666.1 14.3 %conditional.36 = (f32[1,4,6,3840]{3,2,1,0:T(8,128)S(1)}) conditional(s32[]{:T(128)} %convert_element_type.92, f32[4,6,3840]{2,1,0:T(8,128)S(1)} %dynamic-slice_bitcast_fusion.20, (pred[1,4]{1,0:T(4,128)(4,1)S(1)}, s32[3840]{0:T(1024)S(1)}, f32[4,6,3840]{2,1,0:T(8,128)S(1)}, s32[3840]{0:T(1024)S(1)}, f32[6,6]{1,0:T(8,128)S(1)}, ...), branch_computations={%region_25.28_spmd, %region_26.29_spmd.clone} | conditional | flops 7891200 | bytes 13255868 | solution.py:76
  683.7 14.3 %conditional.36 = (f32[1,4,6,3840]{3,2,1,0:T(8,128)S(1)}) conditional(s32[]{:T(128)} %convert_element_type.92, f32[4,6,3840]{2,1,0:T(8,128)S(1)} %dynamic-slice_bitcast_fusion.20, (pred[1,4]{1,0:T(4,128)(4,1)S(1)}, s32[3840]{0:T(1024)S(1)}, f32[4,6,3840]{2,1,0:T(8,128)S(1)}, s32[3840]{0:T(1024)S(1)}, f32[6,6]{1,0:T(8,128)S(1)}, ...), branch_computations={%region_25.28_spmd, %region_26.29_spmd.clone} | conditional | flops 7891200 | bytes 13255868 | solution.py:76
  701.3 14.3 %conditional.36 = (f32[1,4,6,3840]{3,2,1,0:T(8,128)S(1)}) conditional(s32[]{:T(128)} %convert_element_type.92, f32[4,6,3840]{2,1,0:T(8,128)S(1)} %dynamic-slice_bitcast_fusion.20, (pred[1,4]{1,0:T(4,128)(4,1)S(1)}, s32[3840]{0:T(1024)S(1)}, f32[4,6,3840]{2,1,0:T(8,128)S(1)}, s32[3840]{0:T(1024)S(1)}, f32[6,6]{1,0:T(8,128)S(1)}, ...), branch_computations={%region_25.28_spmd, %region_26.29_spmd.clone} | conditional | flops 7891200 | bytes 13255868 | solution.py:76
  718.9 14.3 %conditional.36 = (f32[1,4,6,3840]{3,2,1,0:T(8,128)S(1)}) conditional(s32[]{:T(128)} %convert_element_type.92, f32[4,6,3840]{2,1,0:T(8,128)S(1)} %dynamic-slice_bitcast_fusion.20, (pred[1,4]{1,0:T(4,128)(4,1)S(1)}, s32[3840]{0:T(1024)S(1)}, f32[4,6,3840]{2,1,0:T(8,128)S(1)}, s32[3840]{0:T(1024)S(1)}, f32[6,6]{1,0:T(8,128)S(1)}, ...), branch_computations={%region_25.28_spmd, %region_26.29_spmd.clone} | conditional | flops 7891200 | bytes 13255868 | solution.py:76
  736.5 14.3 %conditional.36 = (f32[1,4,6,3840]{3,2,1,0:T(8,128)S(1)}) conditional(s32[]{:T(128)} %convert_element_type.92, f32[4,6,3840]{2,1,0:T(8,128)S(1)} %dynamic-slice_bitcast_fusion.20, (pred[1,4]{1,0:T(4,128)(4,1)S(1)}, s32[3840]{0:T(1024)S(1)}, f32[4,6,3840]{2,1,0:T(8,128)S(1)}, s32[3840]{0:T(1024)S(1)}, f32[6,6]{1,0:T(8,128)S(1)}, ...), branch_computations={%region_25.28_spmd, %region_26.29_spmd.clone} | conditional | flops 7891200 | bytes 13255868 | solution.py:76
  753.9 83.4 %while.101 = (s32[]{:T(128)}, f32[8,4,6,3840]{3,2,1,0:T(8,128)}, s32[8,4]{1,0:T(8,128)S(1)}, f32[8,4,6,3840]{3,2,1,0:T(8,128)}, f32[6,6]{1,0:T(8,128)S(1)}, /*index=5*/f32[32,6,60]{2,0,1:T(8,128)S(1)}, s32[]{:T(128)}, s32[]{:T(128)}) while((s32[]{:T(128)}, f32[8,4,6,3840]{3,2,1,0:T(8,128)}, s32[8,4]{1,0:T(8,128)S(1)}, ...), condition=%wide.region_32.36_spmd.clone.clone, body=%wide.region_28.35_spmd.clone.clone.sunk | while | flops 7895050 | bytes 15622023 | solution.py:84
  756.3 14.3 %conditional.37 = (f32[1,4,6,3840]{3,2,1,0:T(8,128)S(1)}) conditional(s32[]{:T(128)} %convert_element_type.93, f32[4,6,3840]{2,1,0:T(8,128)S(1)} %dynamic-slice_bitcast_fusion.21, (pred[1,4]{1,0:T(4,128)(4,1)S(1)}, s32[3840]{0:T(1024)S(1)}, f32[4,6,3840]{2,1,0:T(8,128)S(1)}, s32[3840]{0:T(1024)S(1)}, f32[6,6]{1,0:T(8,128)S(1)}, ...), branch_computations={%region_30.33_spmd, %region_31.34_spmd.clone} | conditional | flops 7891200 | bytes 13255868 | solution.py:76
  773.9 14.3 %conditional.37 = (f32[1,4,6,3840]{3,2,1,0:T(8,128)S(1)}) conditional(s32[]{:T(128)} %convert_element_type.93, f32[4,6,3840]{2,1,0:T(8,128)S(1)} %dynamic-slice_bitcast_fusion.21, (pred[1,4]{1,0:T(4,128)(4,1)S(1)}, s32[3840]{0:T(1024)S(1)}, f32[4,6,3840]{2,1,0:T(8,128)S(1)}, s32[3840]{0:T(1024)S(1)}, f32[6,6]{1,0:T(8,128)S(1)}, ...), branch_computations={%region_30.33_spmd, %region_31.34_spmd.clone} | conditional | flops 7891200 | bytes 13255868 | solution.py:76
  791.5 14.3 %conditional.37 = (f32[1,4,6,3840]{3,2,1,0:T(8,128)S(1)}) conditional(s32[]{:T(128)} %convert_element_type.93, f32[4,6,3840]{2,1,0:T(8,128)S(1)} %dynamic-slice_bitcast_fusion.21, (pred[1,4]{1,0:T(4,128)(4,1)S(1)}, s32[3840]{0:T(1024)S(1)}, f32[4,6,3840]{2,1,0:T(8,128)S(1)}, s32[3840]{0:T(1024)S(1)}, f32[6,6]{1,0:T(8,128)S(1)}, ...), branch_computations={%region_30.33_spmd, %region_31.34_spmd.clone} | conditional | flops 7891200 | bytes 13255868 | solution.py:76
  809.1 14.3 %conditional.37 = (f32[1,4,6,3840]{3,2,1,0:T(8,128)S(1)}) conditional(s32[]{:T(128)} %convert_element_type.93, f32[4,6,3840]{2,1,0:T(8,128)S(1)} %dynamic-slice_bitcast_fusion.21, (pred[1,4]{1,0:T(4,128)(4,1)S(1)}, s32[3840]{0:T(1024)S(1)}, f32[4,6,3840]{2,1,0:T(8,128)S(1)}, s32[3840]{0:T(1024)S(1)}, f32[6,6]{1,0:T(8,128)S(1)}, ...), branch_computations={%region_30.33_spmd, %region_31.34_spmd.clone} | conditional | flops 7891200 | bytes 13255868 | solution.py:76
  839.6 69.0 %while.102 = (s32[]{:T(128)}, f32[8,4,6,3840]{3,2,1,0:T(8,128)}, s32[8,4]{1,0:T(8,128)S(1)}, f32[8,4,6,3840]{3,2,1,0:T(8,128)}, f32[6,6]{1,0:T(8,128)S(1)}, /*index=5*/f32[32,6,60]{2,0,1:T(8,128)S(1)}, s32[]{:T(128)}, s32[]{:T(128)}) while((s32[]{:T(128)}, f32[8,4,6,3840]{3,2,1,0:T(8,128)}, s32[8,4]{1,0:T(8,128)S(1)}, ...), condition=%wide.region_37.41_spmd.clone.clone, body=%wide.region_33.40_spmd.clone.clone.sunk | while | flops 7895050 | bytes 15622023 | solution.py:84
  842.1 14.3 %conditional.38 = (f32[1,4,6,3840]{3,2,1,0:T(8,128)S(1)}) conditional(s32[]{:T(128)} %convert_element_type.94, f32[4,6,3840]{2,1,0:T(8,128)S(1)} %dynamic-slice_bitcast_fusion.22, (pred[1,4]{1,0:T(4,128)(4,1)S(1)}, s32[3840]{0:T(1024)S(1)}, f32[4,6,3840]{2,1,0:T(8,128)S(1)}, s32[3840]{0:T(1024)S(1)}, f32[6,6]{1,0:T(8,128)S(1)}, ...), branch_computations={%region_35.38_spmd, %region_36.39_spmd.clone} | conditional | flops 7891200 | bytes 13255868 | solution.py:76
  859.6 14.3 %conditional.38 = (f32[1,4,6,3840]{3,2,1,0:T(8,128)S(1)}) conditional(s32[]{:T(128)} %convert_element_type.94, f32[4,6,3840]{2,1,0:T(8,128)S(1)} %dynamic-slice_bitcast_fusion.22, (pred[1,4]{1,0:T(4,128)(4,1)S(1)}, s32[3840]{0:T(1024)S(1)}, f32[4,6,3840]{2,1,0:T(8,128)S(1)}, s32[3840]{0:T(1024)S(1)}, f32[6,6]{1,0:T(8,128)S(1)}, ...), branch_computations={%region_35.38_spmd, %region_36.39_spmd.clone} | conditional | flops 7891200 | bytes 13255868 | solution.py:76
  877.2 14.3 %conditional.38 = (f32[1,4,6,3840]{3,2,1,0:T(8,128)S(1)}) conditional(s32[]{:T(128)} %convert_element_type.94, f32[4,6,3840]{2,1,0:T(8,128)S(1)} %dynamic-slice_bitcast_fusion.22, (pred[1,4]{1,0:T(4,128)(4,1)S(1)}, s32[3840]{0:T(1024)S(1)}, f32[4,6,3840]{2,1,0:T(8,128)S(1)}, s32[3840]{0:T(1024)S(1)}, f32[6,6]{1,0:T(8,128)S(1)}, ...), branch_computations={%region_35.38_spmd, %region_36.39_spmd.clone} | conditional | flops 7891200 | bytes 13255868 | solution.py:76
  910.9 40.6 %while.103 = (s32[]{:T(128)}, f32[8,4,6,3840]{3,2,1,0:T(8,128)}, s32[8,4]{1,0:T(8,128)S(1)}, f32[8,4,6,3840]{3,2,1,0:T(8,128)}, f32[6,6]{1,0:T(8,128)S(1)}, /*index=5*/f32[32,6,60]{2,0,1:T(8,128)S(1)}, s32[]{:T(128)}, s32[]{:T(128)}) while((s32[]{:T(128)}, f32[8,4,6,3840]{3,2,1,0:T(8,128)}, s32[8,4]{1,0:T(8,128)S(1)}, ...), condition=%wide.region_42.46_spmd.clone.clone, body=%wide.region_38.45_spmd.clone.clone.sunk | while | flops 7895050 | bytes 15622023 | solution.py:84
  913.5 14.3 %conditional.39 = (f32[1,4,6,3840]{3,2,1,0:T(8,128)S(1)}) conditional(s32[]{:T(128)} %convert_element_type.95, f32[4,6,3840]{2,1,0:T(8,128)S(1)} %dynamic-slice_bitcast_fusion.23, (pred[1,4]{1,0:T(4,128)(4,1)S(1)}, s32[3840]{0:T(1024)S(1)}, f32[4,6,3840]{2,1,0:T(8,128)S(1)}, s32[3840]{0:T(1024)S(1)}, f32[6,6]{1,0:T(8,128)S(1)}, ...), branch_computations={%region_40.43_spmd, %region_41.44_spmd.clone} | conditional | flops 7891200 | bytes 13255868 | solution.py:76
  967.3 20.6 %all-to-all-start.8 = ((f32[32,1,72]{2,1,0:T(1,128)}), f32[32,1,72]{2,1,0:T(1,128)S(1)}, u32[]{:S(2)}, u32[]{:S(2)}) async-start(f32[32,1,72]{2,1,0:T(1,128)} %bitcast.81), calls=%async_computation.8 | async-start | bytes 32768 | tf_op jit(solution)/shard_map/all_to_all | solution.py:147
  1006.1 21.5 %collective-permute-done.4 = f32[73,1,32]{0,2,1:T(8,128)S(1)} collective-permute-done((f32[73,1,32]{0,2,1:T(8,128)S(1)}, f32[73,1,32]{0,2,1:T(8,128)S(1)}, u32[]{:S(2)}, u32[]{:S(2)}) %collective-permute-start.4) | collective-permute-done | bytes 9376 | tf_op jit(solution)/shard_map/ppermute | solution.py:23
  1028.3 28.1 %collective-permute-start.6 = (f32[73,3,1]{0,2,1:T(1,128)S(1)}, f32[73,3,1]{0,2,1:T(1,128)S(1)}, u32[]{:S(2)}, u32[]{:S(2)}) collective-permute-start(f32[73,3,1]{0,2,1:T(1,128)S(1)} %get-tuple-element.1586), channel_id=1, source_target_pairs={{0,1},{1,2},{2,3},{3,0},{4,5},{5,6},{6,7},{7,4},{8,9},{9,10},{10,1... | collective-permute-start | bytes 2636 | tf_op jit(solution)/shard_map/ppermute | solution.py:23
  1057.7 29.2 %collective-permute-done.7 = f32[73,3,1]{0,2,1:T(1,128)S(1)} collective-permute-done((f32[73,3,1]{0,2,1:T(1,128)S(1)}, f32[73,3,1]{0,2,1:T(1,128)S(1)}, u32[]{:S(2)}, u32[]{:S(2)}) %collective-permute-start.7) | collective-permute-done | bytes 908 | tf_op jit(solution)/shard_map/ppermute | solution.py:26
  (863 shorter events, 788.0 us)
Async XLA Ops:
  0.6 451.1 %copy-start = (f32[72,60]{0,1:T(8,128)S(1)}, f32[72,60]{0,1:T(8,128)}, u32[]{:S(2)}) copy-start(f32[72,60]{0,1:T(8,128)} %param.54) | copy-start | bytes 51844
  16.8 11.1 %all-to-all-start.2 = ((f32[32,1,72]{2,1,0:T(1,128)}), f32[32,1,72]{2,1,0:T(1,128)S(1)}, u32[]{:S(2)}, u32[]{:S(2)}) async-start(f32[32,1,72]{2,1,0:T(1,128)} %bitcast.422), calls=%async_computation.2 | async-start | bytes 32768 | tf_op jit(solution)/shard_map/all_to_all | solution.py:134
  24.8 8.0 copy-start.22
  24.8 8.1 copy-start.11
  24.8 18.6 %copy-start.12 = (f32[60,72]{1,0:T(8,128)S(1)}, f32[60,72]{1,0:T(8,128)}, u32[]{:S(2)}) copy-start(f32[60,72]{1,0:T(8,128)} %param.52) | copy-start | bytes 51844
  24.8 57.7 %copy-start.18 = (f32[6]{0:T(128)S(1)}, f32[6]{0:T(128)}, u32[]{:S(2)}) copy-start(f32[6]{0:T(128)} %param.53) | copy-start | bytes 76
  27.9 56.7 %all-to-all-start.1 = ((f32[32,6,3840]{2,1,0:T(8,128)}), f32[32,6,3840]{2,1,0:T(8,128)}, u32[]{:S(2)}, u32[]{:S(2)}) async-start(f32[32,6,3840]{2,1,0:T(8,128)} %bitcast_convert_fusion), calls=%async_computation.1 | async-start | bytes 7864320 | tf_op jit(solution)/shard_map/all_to_all | solution.py:133
  32.9 446.1 %copy-start.9 = (f32[1,1,32]{0,2,1:T(8,128)}, f32[1,1,32]{0,2,1:T(8,128)S(1)}, u32[]{:S(2)}) copy-start(f32[1,1,32]{0,2,1:T(8,128)S(1)} %copy.59) | copy-start | bytes 388
  32.9 46.2 %collective-permute-start = (f32[73,1,32]{0,2,1:T(8,128)S(1)}, f32[73,1,32]{0,2,1:T(8,128)S(1)}, u32[]{:S(2)}, u32[]{:S(2)}) collective-permute-start(f32[73,1,32]{0,2,1:T(8,128)S(1)} %pad_maximum_fusion.20), channel_id=1, source_target_pairs={{0,4},{4,8},{8,12},{12,16},{16,20},{20,24},{24,28},{28,32},{32,36}... | collective-permute-start | bytes 28040 | tf_op jit(solution)/shard_map/ppermute | solution.py:23
  33.0 46.1 %collective-permute-start.1 = (f32[73,1,32]{0,2,1:T(8,128)S(1)}, f32[73,1,32]{0,2,1:T(8,128)S(1)}, u32[]{:S(2)}, u32[]{:S(2)}) collective-permute-start(f32[73,1,32]{0,2,1:T(8,128)S(1)} %pad_maximum_fusion.20), channel_id=1, source_target_pairs={{4,0},{8,4},{12,8},{16,12},{20,16},{24,20},{28,24},{32,28},{36,32}... | collective-permute-start | bytes 28040 | tf_op jit(solution)/shard_map/ppermute | solution.py:26
  40.3 49.2 %copy-start.14 = (s32[1024]{0:T(1024)}, s32[1024]{0:T(1024)S(1)}, u32[]{:S(2)}) copy-start(s32[1024]{0:T(1024)S(1)} %pad_clamp_fusion.1) | copy-start | bytes 12292
  42.7 429.0 %copy-start.15 = (s32[1024]{0:T(1024)}, s32[1024]{0:T(1024)S(1)}, u32[]{:S(2)}) copy-start(s32[1024]{0:T(1024)S(1)} %pad_clamp_fusion) | copy-start | bytes 12292
  42.8 441.8 %copy-start.16 = (pred[32]{0:T(512)(128)(4,1)}, pred[32]{0:T(512)(128)(4,1)S(1)}, u32[]{:S(2)}) copy-start(pred[32]{0:T(512)(128)(4,1)S(1)} %compare_and_fusion.8) | copy-start | bytes 100
  79.3 4.8 collective-permute-start.2
  80.9 3.6 collective-permute-start.3
  94.1 2.3 copy-start.23
  99.1 0.8 copy-start.1
  116.7 0.8 copy-start.1
  151.8 0.8 copy-start.1
  169.5 0.8 copy-start.1
  187.0 0.8 copy-start.1
  204.6 0.8 copy-start.1
  259.6 0.8 copy-start.2
  327.8 0.8 copy-start.3
  345.3 0.8 copy-start.3
  399.0 0.8 copy-start.4
  446.9 4.5 copy-start.20
  453.2 25.7 %all-to-all-start.5 = ((f32[32,1,72]{2,1,0:T(1,128)}), f32[32,1,72]{2,1,0:T(1,128)S(1)}, u32[]{:S(2)}, u32[]{:S(2)}) async-start(f32[32,1,72]{2,1,0:T(1,128)} %bitcast.61), calls=%async_computation.5 | async-start | bytes 32768 | tf_op jit(solution)/shard_map/all_to_all | solution.py:141
  479.6 12.3 %all-to-all-start.6 = ((f32[32,1,72]{2,1,0:T(1,128)}), f32[32,1,72]{2,1,0:T(1,128)S(1)}, u32[]{:S(2)}, u32[]{:S(2)}) async-start(f32[32,1,72]{2,1,0:T(1,128)} %bitcast.73), calls=%async_computation.6 | async-start | bytes 32768 | tf_op jit(solution)/shard_map/all_to_all | solution.py:134
  544.3 5.8 copy-start.13
  544.3 6.1 copy-start.19
  544.3 54.8 %all-to-all-start.4 = ((f32[32,6,3840]{2,1,0:T(8,128)}), f32[32,6,3840]{2,1,0:T(8,128)}, u32[]{:S(2)}, u32[]{:S(2)}) async-start(f32[32,6,3840]{2,1,0:T(8,128)} %all_to_all.76), calls=%async_computation.4 | async-start | bytes 7864320 | tf_op jit(solution)/shard_map/all_to_all | solution.py:133
  613.3 0.8 copy-start.5
  648.5 0.8 copy-start.5
  683.7 0.8 copy-start.5
  736.5 0.8 copy-start.5
  756.3 0.8 copy-start.6
  773.9 0.8 copy-start.6
  791.5 0.8 copy-start.6
  960.9 4.5 copy-start.21
  960.9 5.7 copy-start.17
  967.3 27.9 %all-to-all-start.8 = ((f32[32,1,72]{2,1,0:T(1,128)}), f32[32,1,72]{2,1,0:T(1,128)S(1)}, u32[]{:S(2)}, u32[]{:S(2)}) async-start(f32[32,1,72]{2,1,0:T(1,128)} %bitcast.81), calls=%async_computation.8 | async-start | bytes 32768 | tf_op jit(solution)/shard_map/all_to_all | solution.py:147
  990.9 9.2 copy-start.10
  995.3 94.1 %all-to-all-start.7 = ((bf16[32,6,3840]{2,1,0:T(8,128)(2,1)}), bf16[32,6,3840]{2,1,0:T(8,128)(2,1)S(1)}, u32[]{:S(2)}, u32[]{:S(2)}) async-start(bf16[32,6,3840]{2,1,0:T(8,128)(2,1)} %select_convert_fusion), calls=%async_computation.7 | async-start | bytes 3932160 | tf_op jit(solution)/shard_map/all_to_all | solution.py:144
  1001.0 26.5 %collective-permute-start.4 = (f32[73,1,32]{0,2,1:T(8,128)S(1)}, f32[73,1,32]{0,2,1:T(8,128)S(1)}, u32[]{:S(2)}, u32[]{:S(2)}) collective-permute-start(f32[73,1,32]{0,2,1:T(8,128)S(1)} %pad_maximum_fusion.21), channel_id=1, source_target_pairs={{0,4},{4,8},{8,12},{12,16},{16,20},{20,24},{24,28},{28,32},{32,36}... | collective-permute-start | bytes 28040 | tf_op jit(solution)/shard_map/ppermute | solution.py:23
  1001.3 26.3 %collective-permute-start.5 = (f32[73,1,32]{0,2,1:T(8,128)S(1)}, f32[73,1,32]{0,2,1:T(8,128)S(1)}, u32[]{:S(2)}, u32[]{:S(2)}) collective-permute-start(f32[73,1,32]{0,2,1:T(8,128)S(1)} %pad_maximum_fusion.21), channel_id=1, source_target_pairs={{4,0},{8,4},{12,8},{16,12},{20,16},{24,20},{28,24},{32,28},{36,32}... | collective-permute-start | bytes 28040 | tf_op jit(solution)/shard_map/ppermute | solution.py:26
  1028.3 29.4 %collective-permute-start.6 = (f32[73,3,1]{0,2,1:T(1,128)S(1)}, f32[73,3,1]{0,2,1:T(1,128)S(1)}, u32[]{:S(2)}, u32[]{:S(2)}) collective-permute-start(f32[73,3,1]{0,2,1:T(1,128)S(1)} %get-tuple-element.1586), channel_id=1, source_target_pairs={{0,1},{1,2},{2,3},{3,0},{4,5},{5,6},{6,7},{7,4},{8,9},{9,10},{10,1... | collective-permute-start | bytes 2636 | tf_op jit(solution)/shard_map/ppermute | solution.py:23
  1056.4 30.5 %collective-permute-start.7 = (f32[73,3,1]{0,2,1:T(1,128)S(1)}, f32[73,3,1]{0,2,1:T(1,128)S(1)}, u32[]{:S(2)}, u32[]{:S(2)}) collective-permute-start(f32[73,3,1]{0,2,1:T(1,128)S(1)} %get-tuple-element.1585), channel_id=1, source_target_pairs={{1,0},{2,1},{3,2},{0,3},{5,4},{6,5},{7,6},{4,7},{9,8},{10,9},{11,1... | collective-permute-start | bytes 2636 | tf_op jit(solution)/shard_map/ppermute | solution.py:26
  (15 other events, 11.7 us)
where the time goes:
time: 1100 us; the launch traced here: 1090 us
  local copies, waits for them, and re-layouts  486 us (44%)
  waiting for transfers between devices  149 us (14%)
  matrix products  145 us (13%)
  starting transfers between devices  104 us (9%)
  other arithmetic  91.6 us (8%)
  blocking collectives  67.7 us (6%)
  loops' own time  46.6 us (4%)
    another operation x32, local copies, waits for them, and re-layouts, cloud_run(): forcing_cells.reshape((nblocks, block) + forcing_cells.shape[1:])  166 us
    dot_general x32, matrix products, cloud_substep(): jnp.einsum('fg,bgp->bfp', coupling, fields, precision=highest)  144 us
    broadcast_in_dim x32, local copies, waits for them, and re-layouts, cloud_run(): forcing_cells = jnp.repeat(forcing, NXC, axis=-1)  122 us
    squeeze x64, local copies, waits for them, and re-layouts, cloud_run(): lax.scan(advance, 0, (field_blocks, force_blocks, count_blocks))  68 us
    ppermute x4, waiting for transfers between devices, extended_2(): lax.ppermute(lax.slice_in_dim(block, block.shape[dim] - width, None, axis...  59.8 us
    dynamic_update_slice x64, local copies, waits for them, and re-layouts, cloud_run(): lax.scan(advance, 0, (field_blocks, force_blocks, count_blocks))  53.4 us
    all_to_all x1, blocking collectives, body(): lax.all_to_all(moved, 'elem', split_axis=0, concat_axis=0, tiled=True)  52.4 us
    all_to_all x2, waiting for transfers between devices, body(): lax.all_to_all(state, 'elem', split_axis=0, concat_axis=0, tiled=True)  48.6 us
  transfers between devices with their start and end apart: 15, of which 11 were waited for; matrix products, arithmetic and copies ran while one was open for 3% of the time, Pallas kernels for 0%

commit v1 on v0

v1 whole, which is shorter than its diff:
```python
import jax
import jax.numpy as jnp
from jax import lax
from jax.experimental import pallas as pl
from jax.experimental.pallas import tpu as pltpu
from jax.sharding import PartitionSpec as P

LEV = 72
FIELDS = 6
NZC = 60
NXC = 64
SUB = 4
WINDOWS = 2
COLS = 32
ROWS = FIELDS * COLS
BLOCKS = 15
LANES = 256
TILES = 30
CELLS = NZC * NXC
STEP = 0.1
MESH = pl.DeviceIdType.MESH
F32 = jnp.float32
BF16 = jnp.bfloat16
HIGHEST = lax.Precision.HIGHEST
NT = (((1,), (1,)), ((), ()))


def iota(shape, axis):
    return lax.broadcasted_iota(jnp.int32, shape, axis)


def to_column(row):
    eye = iota((COLS, COLS), 0) == iota((COLS, COLS), 1)
    return jnp.sum(jnp.where(eye, jnp.broadcast_to(row, (COLS, COLS)), 0.0), axis=1, keepdims=True)


def swap_halves(tile):
    return pltpu.roll(tile, 64, 1)


def kernel(
    crm_in, host_in, kappa_in, counts_in, level_in, back_in, coup, scale, weight,
    crm_out, host_out,
    xbuf, obuf, sa, sb, force, qsum, kron, deriv, level2, back2, host, halo_e, halo_b,
    in_sem, out_sem, send_sem, recv_sem,
):
    elem, band = lax.axis_index("elem"), lax.axis_index("band")
    n_elem, n_band = lax.axis_size("elem"), lax.axis_size("band")
    up_e = (lax.rem(elem + 1, n_elem), band)
    dn_e = (lax.rem(elem + n_elem - 1, n_elem), band)
    up_b = (elem, lax.rem(band + 1, n_band))
    dn_b = (elem, lax.rem(band + n_band - 1, n_band))

    barrier = pltpu.get_barrier_semaphore()
    for other in (up_e, dn_e, up_b, dn_b):
        pl.semaphore_signal(barrier, inc=1, device_id=other, device_id_type=MESH)

    loads = [pltpu.make_async_copy(crm_in.at[f], xbuf.at[f], in_sem.at[f]) for f in range(FIELDS)]
    for copy in loads:
        copy.start()

    kcol = to_column(kappa_in[...])
    ccol = to_column(counts_in[...].astype(F32))
    lane = iota((COLS, 128), 1)
    host[0] = jnp.where(lane == LEV, jnp.broadcast_to(kcol, (COLS, 128)), 0.0)
    host[0, :, 0:LEV] = host_in[...]

    pl.semaphore_wait(barrier, 4)

    def exchange(window):
        src = host.at[window]
        copies = []
        for i, (other, part, dst) in enumerate((
            (up_e, src, halo_e.at[window, 0]),
            (dn_e, src, halo_e.at[window, 1]),
            (up_b, src.at[pl.ds(COLS - 8, 8)], halo_b.at[window, 0]),
            (dn_b, src.at[pl.ds(0, 8)], halo_b.at[window, 1]),
        )):
            copies.append(pltpu.make_async_remote_copy(
                src_ref=part, dst_ref=dst,
                send_sem=send_sem.at[window, i], recv_sem=recv_sem.at[window, i],
                device_id=other, device_id_type=MESH,
            ))
        return copies

    copies = exchange(0)
    for copy in copies:
        copy.start()

    level2[...] = jnp.zeros_like(level2)
    level2[0:NZC, :] = level_in[...]
    level2[64 : 64 + NZC, :] = level_in[...]
    back2[...] = jnp.zeros_like(back2)
    back2[0:LEV, 0:NZC] = back_in[...]
    row_c = iota((COLS, ROWS), 0)
    lane_r = iota((COLS, ROWS), 1)
    for f in range(FIELDS):
        value = jnp.zeros((COLS, ROWS), F32)
        for g in range(FIELDS):
            value = jnp.where(lane_r == row_c + g * COLS, coup[f, g], value)
        kron[f * COLS : (f + 1) * COLS, :] = value.astype(BF16)
    src = iota((LANES, LANES), 0)
    dst = iota((LANES, LANES), 1)
    same = (src // NXC) == (dst // NXC)
    ahead = jnp.logical_and(same, (src % NXC) == (dst + 1) % NXC)
    behind = jnp.logical_and(same, (dst % NXC) == (src + 1) % NXC)
    deriv[...] = (jnp.where(behind, 0.5, 0.0) - jnp.where(ahead, 0.5, 0.0)).astype(BF16)

    low = iota((COLS, 128), 1) < NXC
    for f in range(FIELDS):
        loads[f].wait()
        rows = slice(f * COLS, (f + 1) * COLS)
        for j in range(BLOCKS):
            for half in range(2):
                za, zb = 30 * half + j, 30 * half + 15 + j
                ta = xbuf[f, :, (za // 2) * 128 : (za // 2 + 1) * 128]
                tb = xbuf[f, :, (zb // 2) * 128 : (zb // 2 + 1) * 128]
                if j % 2 == 0:
                    tile = jnp.where(low, ta, tb)
                else:
                    tile = swap_halves(jnp.where(low, tb, ta))
                sa[j, rows, half * 128 : (half + 1) * 128] = tile.astype(F32)

    def weighted(j):
        total = weight[0] * sa[j, 0:COLS, :]
        for f in range(1, FIELDS):
            total = total + weight[f] * sa[j, f * COLS : (f + 1) * COLS, :]
        return total

    for j in range(BLOCKS):
        qsum[j] = weighted(j)

    lane_q = iota((COLS, LANES), 1)

    def shift_up(value):
        moved = pltpu.roll(value, NXC, 1)
        return jnp.where(lane_q < NXC, 0.0, moved)

    def shift_down(value):
        moved = pltpu.roll(value, LANES - NXC, 1)
        return jnp.where(lane_q >= LANES - NXC, 0.0, moved)

    cnt = jnp.broadcast_to(ccol, (COLS, LANES))

    def substep(src_ref, dst_ref, turn):
        a = jnp.where(cnt > turn.astype(F32), STEP, 0.0)
        keep = 1.0 - 2.0 * a
        for j in range(BLOCKS):
            state = src_ref[j]
            packed = state.astype(BF16)
            mix = jnp.dot(kron[...], packed, preferred_element_type=F32)
            slope = jnp.dot(packed, deriv[...], preferred_element_type=F32)
            wind = state[0:COLS]
            for f in range(FIELDS):
                rows = slice(f * COLS, (f + 1) * COLS)
                above = src_ref[j + 1, rows] if j < BLOCKS - 1 else shift_down(src_ref[0, rows])
                below = src_ref[j - 1, rows] if j > 0 else shift_up(src_ref[BLOCKS - 1, rows])
                total = (above + below) + (jnp.tanh(mix[rows]) + force[j, rows]) + wind * slope[rows]
                dst_ref[j, rows] = keep * state[rows] + a * total

    zq = iota((128, LANES), 0)
    lq = iota((128, LANES), 1)
    spread_lanes = jnp.where((zq % 64) == 15 * (lq // NXC), 1.0, 0.0).astype(BF16)
    rq = iota((LANES, 128), 0)
    cq = iota((LANES, 128), 1)
    gather_lanes = jnp.where(cq == 15 * (rq // NXC), 1.0 / NXC, 0.0).astype(BF16)
    sub_row = iota((COLS, 128), 0)

    for window in range(WINDOWS):
        hval = host[window]
        mapped = lax.dot_general(hval[:, 0:LEV], level2[...], NT, precision=HIGHEST, preferred_element_type=F32)
        high = mapped.astype(BF16).astype(F32)
        mhl = jnp.where(lane < 64, high, mapped - high)
        stack = jnp.concatenate([mhl] + [pltpu.roll(mhl, 128 - j, 1) for j in range(1, BLOCKS)], axis=0)
        cells = jnp.dot(stack.astype(BF16), spread_lanes, preferred_element_type=F32)
        for j in range(BLOCKS):
            for f in range(FIELDS):
                force[j, f * COLS : (f + 1) * COLS, :] = scale[f] * cells[j * COLS : (j + 1) * COLS, :]

        def turns(i, carry):
            substep(sa, sb, 2 * i)
            substep(sb, sa, 2 * i + 1)
            return carry

        lax.fori_loop(0, SUB // 2, turns, 0)

        parts = []
        for j in range(BLOCKS):
            now = weighted(j)
            parts.append((now - qsum[j]).astype(BF16))
            qsum[j] = now
        means = jnp.dot(jnp.concatenate(parts, axis=0), gather_lanes, preferred_element_type=F32)
        mixed = means[0:COLS]
        for j in range(1, BLOCKS):
            mixed = mixed + pltpu.roll(means[j * COLS : (j + 1) * COLS], j, 1)
        tend = lax.dot_general(mixed, back2[...], NT, precision=HIGHEST, preferred_element_type=F32)

        for copy in copies:
            copy.wait()
        kmid = jnp.broadcast_to(kcol, (COLS, 128))

        def face(near):
            knear = jnp.broadcast_to(near[:, LEV : LEV + 1], (COLS, 128))
            return 0.5 * (kmid + knear) * (near - hval)

        prev = pltpu.roll(hval, 1, 0)
        prev = jnp.where(sub_row == 0, jnp.broadcast_to(halo_b[window, 0, 7:8, :], (COLS, 128)), prev)
        nxt = pltpu.roll(hval, COLS - 1, 0)
        nxt = jnp.where(sub_row == COLS - 1, jnp.broadcast_to(halo_b[window, 1, 0:1, :], (COLS, 128)), nxt)
        flux = face(halo_e[window, 1]) + face(halo_e[window, 0])
        flux = flux + face(nxt) + face(prev)
        hnew = hval + (tend + flux)
        if window < WINDOWS - 1:
            host[window + 1] = jnp.where(lane == LEV, kmid, hnew)
            copies = exchange(window + 1)
            for copy in copies:
                copy.start()
        else:
            host_out[...] = hnew[:, 0:LEV]

    stores = [pltpu.make_async_copy(obuf.at[f], crm_out.at[f], out_sem.at[f]) for f in range(FIELDS)]
    for f in range(FIELDS):
        rows = slice(f * COLS, (f + 1) * COLS)
        tiles = {}
        for j in range(BLOCKS):
            for half in range(2):
                tile = sa[j, rows, half * 128 : (half + 1) * 128].astype(BF16)
                tiles[j, half] = tile if j % 2 == 0 else swap_halves(tile)
        for t in range(TILES):
            za, zb = 2 * t, 2 * t + 1
            ta = tiles[za % 15, za // 30]
            tb = tiles[zb % 15, zb // 30]
            obuf[f, :, t * 128 : (t + 1) * 128] = jnp.where(low, ta, tb)
        stores[f].start()
    for copy in stores:
        copy.wait()


def body(
    crm_state, host_state, kappa, substeps, coupling, level_map, field_scale, back_map, back_weight
):
    crm = jnp.transpose(crm_state[0], (1, 0, 2))
    host = jnp.transpose(host_state[:, 0, :], (1, 0))
    vmem = pl.BlockSpec(memory_space=pltpu.VMEM)
    smem = pl.BlockSpec(memory_space=pltpu.SMEM)
    anym = pl.BlockSpec(memory_space=pl.ANY)
    crm_final, host_final = pl.pallas_call(
        kernel,
        out_shape=(
            jax.ShapeDtypeStruct((FIELDS, COLS, CELLS), BF16),
            jax.ShapeDtypeStruct((COLS, LEV), F32),
        ),
        in_specs=[anym, vmem, vmem, vmem, vmem, vmem, smem, smem, smem],
        out_specs=(anym, vmem),
        scratch_shapes=[
            pltpu.VMEM((FIELDS, COLS, CELLS), BF16),
            pltpu.VMEM((FIELDS, COLS, CELLS), BF16),
            pltpu.VMEM((BLOCKS, ROWS, LANES), F32),
            pltpu.VMEM((BLOCKS, ROWS, LANES), F32),
            pltpu.VMEM((BLOCKS, ROWS, LANES), F32),
            pltpu.VMEM((BLOCKS, COLS, LANES), F32),
            pltpu.VMEM((ROWS, ROWS), BF16),
            pltpu.VMEM((LANES, LANES), BF16),
            pltpu.VMEM((128, LEV), F32),
            pltpu.VMEM((128, 128), F32),
            pltpu.VMEM((WINDOWS, COLS, 128), F32),
            pltpu.VMEM((WINDOWS, 2, COLS, 128), F32),
            pltpu.VMEM((WINDOWS, 2, 8, 128), F32),
            pltpu.SemaphoreType.DMA((FIELDS,)),
            pltpu.SemaphoreType.DMA((FIELDS,)),
            pltpu.SemaphoreType.DMA((WINDOWS, 4)),
            pltpu.SemaphoreType.DMA((WINDOWS, 4)),
        ],
        compiler_params=pltpu.CompilerParams(
            collective_id=0, has_side_effects=True, vmem_limit_bytes=48 * 1024 * 1024
        ),
    )(crm, host, kappa, substeps, level_map, back_map, coupling, field_scale, back_weight)
    return (
        jnp.transpose(crm_final, (1, 0, 2))[None],
        jnp.transpose(host_final, (1, 0))[:, None, :],
    )


def solution(mesh):
    return jax.shard_map(
        body,
        mesh=mesh,
        in_specs=(
            P("elem", "band", None, None),
            P(None, "elem", "band"),
            P("elem", "band"),
            P("elem", "band"),
            P(),
            P(),
            P(),
            P(),
            P(),
        ),
        out_specs=(P("elem", "band", None, None), P(None, "elem", "band")),
        check_vma=False,
    )
```

time: 1100 us -> 33.6 us (0.03)
  local copies, waits for them, and re-layouts: 486 us -> 8.71 us
  waiting for transfers between devices: 149 us -> 0 us
  matrix products: 145 us -> 0 us
  starting transfers between devices: 104 us -> 0 us
  other arithmetic: 91.6 us -> 0 us
  blocking collectives: 67.7 us -> 0 us
  loops' own time: 46.6 us -> 0 us
  Pallas kernels: 0 us -> 23.8 us
    another operation x104 -> x0, local copies, waits for them, and re-layouts: 185 us -> none  [the longest x32 166 us: cloud_run(): forcing_cells.reshape((nblocks, block) + forcing_cells.shape[1:])]
    dot_general x38 -> x0, matrix products: 145 us -> none  [the longest x32 144 us: cloud_substep(): jnp.einsum('fg,bgp->bfp', coupling, fields, precision=highest)]
    broadcast_in_dim x33 -> x0, local copies, waits for them, and re-layouts: 122 us -> none  [the longest x32 122 us: cloud_run(): forcing_cells = jnp.repeat(forcing, NXC, axis=-1)]
    ppermute x8 -> x0, waiting for transfers between devices: 89.4 us -> none  [the longest x4 59.8 us: extended_2(): lax.ppermute(lax.slice_in_dim(block, block.shape[dim] - width, None, axis...]
    squeeze x64 -> x0, local copies, waits for them, and re-layouts: 68 us -> none  [cloud_run(): lax.scan(advance, 0, (field_blocks, force_blocks, count_blocks))]
    all_to_all x2 -> x0, blocking collectives: 67.7 us -> none  [the longest x1 52.4 us: body(): lax.all_to_all(moved, 'elem', split_axis=0, concat_axis=0, tiled=True)]
    all_to_all x7 -> x0, starting transfers between devices: 62.8 us -> none  [the longest x1 20.6 us: body(): tend = lax.all_to_all(tend, 'elem', split_axis=0, concat_axis=0, tiled=True)]
    all_to_all x7 -> x0, waiting for transfers between devices: 59.5 us -> none  [the longest x2 48.6 us: body(): lax.all_to_all(state, 'elem', split_axis=0, concat_axis=0, tiled=True)]
  transfers between devices with their start and end apart: 15 -> 0, of which waited for: 11 -> 0; matrix products, arithmetic and copies ran while one was open for 3% -> 0% of each run, Pallas kernels for 0% -> 0%
where the time goes in v1:
time: 33.6 us; the launch traced here: 33.2 us
  Pallas kernels  23.8 us (71%)
  local copies, waits for them, and re-layouts  8.71 us (26%)
  between operations  0.65 us (2%)
    pallas_call x1, Pallas kernels, body(): pl.pallas_call(kernel, out_shape=(jax.ShapeDtypeStruct((FIELDS, COLS, CEL...  23.8 us
    unnamed x19, local copies, waits for them, and re-layouts  8.71 us

profile of v1, /device:TPU:0, one launch (start us, length us, event | category | flops | bytes accessed | tf_op | source)
XLA Modules:
  0.0 33.2 jit_solution(1586450820607898832)
XLA Ops:
  0.6 0.8 %copy.11.back_in = f32[72,60]{1,0:T(8,128)S(1)} copy(f32[72,60]{0,1:T(8,128)} %param.16) | data formatting | bytes 34560 | tf_op args[7]
  1.5 0.0 copy-start
  1.5 1.4 %copy-done = bf16[1,32,6,3840]{3,1,2,0:T(8,128)(2,1)S(1)} copy-done((bf16[1,32,6,3840]{3,1,2,0:T(8,128)(2,1)S(1)}, bf16[1,32,6,3840]{3,1,2,0:T(8,128)(2,1)}, u32[]{:S(2)}) %copy-start) | copy-done | bytes 1474584
  2.8 0.0 copy-start.1
  2.9 0.8 %copy-done.1 = f32[60,72]{1,0:T(8,128)S(1)} copy-done((f32[60,72]{1,0:T(8,128)S(1)}, f32[60,72]{1,0:T(8,128)}, u32[]{:S(2)}) %copy-start.1) | copy-done | bytes 17304
  3.6 0.0 copy-start.2
  3.6 0.7 %copy-done.2 = f32[72,1,32]{0,2,1:T(8,128)S(1)} copy-done((f32[72,1,32]{0,2,1:T(8,128)S(1)}, f32[72,1,32]{0,2,1:T(8,128)}, u32[]{:S(2)}) %copy-start.2) | copy-done | bytes 9240
  4.3 0.0 copy-start.3
  4.3 0.7 %copy-done.3 = f32[6,6]{1,0:T(8,128)S(1)} copy-done((f32[6,6]{1,0:T(8,128)S(1)}, f32[6,6]{1,0:T(8,128)}, u32[]{:S(2)}) %copy-start.3) | copy-done | bytes 168
  5.0 0.0 copy-start.4
  5.0 0.7 %copy-done.4 = f32[1,32]{1,0:T(1,128)S(1)} copy-done((f32[1,32]{1,0:T(1,128)S(1)}, f32[1,32]{1,0:T(1,128)}, u32[]{:S(2)}) %copy-start.4) | copy-done | bytes 152
  5.7 0.0 copy-start.5
  5.7 0.7 %copy-done.5 = s32[1,32]{1,0:T(1,128)S(1)} copy-done((s32[1,32]{1,0:T(1,128)S(1)}, s32[1,32]{1,0:T(1,128)}, u32[]{:S(2)}) %copy-start.5) | copy-done | bytes 152
  6.3 0.0 copy-start.6
  6.3 0.7 %copy-done.6 = f32[6]{0:T(128)S(1)} copy-done((f32[6]{0:T(128)S(1)}, f32[6]{0:T(128)}, u32[]{:S(2)}) %copy-start.6) | copy-done | bytes 48
  7.0 0.0 copy-start.7
  7.0 0.7 %copy-done.7 = f32[6]{0:T(128)S(1)} copy-done((f32[6]{0:T(128)S(1)}, f32[6]{0:T(128)}, u32[]{:S(2)}) %copy-start.7) | copy-done | bytes 48
  7.6 23.8 %shard_map.104 = (bf16[6,32,3840]{2,1,0:T(8,128)(2,1)S(1)}, f32[32,72]{1,0:T(8,128)S(1)}) custom-call(bf16[6,32,3840]{2,1,0:T(8,128)(2,1)S(1)} %bitcast.12, f32[32,72]{1,0:T(8,128)S(1)} %bitcast.14, f32[1,32]{1,0:T(1,128)S(1)} %copy-done.4, s32[1,32]{1,0:T(1,128)S(1)} %copy-done.5, f32[60,72]{1,0:T(8,128)S(1)} %copy-done.1, f32[72,60]{1,0:T(8,128)S(1)} %copy.11.back_in, ...), custom_call_target="tpu_custom_call" | custom-call | tf_op jit(solution)/shard_map/pallas_call | solution.py:247
  31.5 1.1 %copy.14 = bf16[1,32,6,3840]{3,1,2,0:T(8,128)(2,1)} copy(bf16[1,32,6,3840]{3,1,2,0:T(8,128)(2,1)S(1)} %bitcast.13) | data formatting | bytes 2949120
  32.6 0.6 %copy.15 = f32[72,1,32]{0,2,1:T(8,128)} copy(f32[72,1,32]{0,2,1:T(8,128)S(1)} %bitcast.15) | data formatting | bytes 18432
Async XLA Ops:
  1.5 1.4 %copy-start = (bf16[1,32,6,3840]{3,1,2,0:T(8,128)(2,1)S(1)}, bf16[1,32,6,3840]{3,1,2,0:T(8,128)(2,1)}, u32[]{:S(2)}) copy-start(bf16[1,32,6,3840]{3,1,2,0:T(8,128)(2,1)} %param.9) | copy-start | bytes 4423684
  2.8 0.8 %copy-start.1 = (f32[60,72]{1,0:T(8,128)S(1)}, f32[60,72]{1,0:T(8,128)}, u32[]{:S(2)}) copy-start(f32[60,72]{1,0:T(8,128)} %level_in.1) | copy-start | bytes 51844
  3.6 0.7 %copy-start.2 = (f32[72,1,32]{0,2,1:T(8,128)S(1)}, f32[72,1,32]{0,2,1:T(8,128)}, u32[]{:S(2)}) copy-start(f32[72,1,32]{0,2,1:T(8,128)} %param.10) | copy-start | bytes 27652
  4.3 0.7 %copy-start.3 = (f32[6,6]{1,0:T(8,128)S(1)}, f32[6,6]{1,0:T(8,128)}, u32[]{:S(2)}) copy-start(f32[6,6]{1,0:T(8,128)} %coup.1) | copy-start | bytes 436
  5.0 0.7 %copy-start.4 = (f32[1,32]{1,0:T(1,128)S(1)}, f32[1,32]{1,0:T(1,128)}, u32[]{:S(2)}) copy-start(f32[1,32]{1,0:T(1,128)} %kappa_in.1) | copy-start | bytes 388
  5.7 0.7 %copy-start.5 = (s32[1,32]{1,0:T(1,128)S(1)}, s32[1,32]{1,0:T(1,128)}, u32[]{:S(2)}) copy-start(s32[1,32]{1,0:T(1,128)} %counts_in.1) | copy-start | bytes 388
  6.3 0.7 %copy-start.6 = (f32[6]{0:T(128)S(1)}, f32[6]{0:T(128)}, u32[]{:S(2)}) copy-start(f32[6]{0:T(128)} %scale.1) | copy-start | bytes 76
  7.0 0.7 %copy-start.7 = (f32[6]{0:T(128)S(1)}, f32[6]{0:T(128)}, u32[]{:S(2)}) copy-start(f32[6]{0:T(128)} %weight.1) | copy-start | bytes 76

commit v2 on v1

v2 whole, which is shorter than its diff:
```python
import jax
import jax.numpy as jnp
from jax import lax
from jax.experimental import pallas as pl
from jax.experimental.pallas import tpu as pltpu
from jax.sharding import PartitionSpec as P

LEV = 72
FIELDS = 6
NZC = 60
NXC = 64
SUB = 4
WINDOWS = 2
COLS = 32
ROWS = FIELDS * COLS
BLOCKS = 15
LANES = 256
TILES = 30
CELLS = NZC * NXC
STEP = 0.1
MESH = pl.DeviceIdType.MESH
F32 = jnp.float32
BF16 = jnp.bfloat16
HIGHEST = lax.Precision.HIGHEST
NT = (((1,), (1,)), ((), ()))


def iota(shape, axis):
    return lax.broadcasted_iota(jnp.int32, shape, axis)


def to_column(row):
    eye = iota((COLS, COLS), 0) == iota((COLS, COLS), 1)
    return jnp.sum(jnp.where(eye, jnp.broadcast_to(row, (COLS, COLS)), 0.0), axis=1, keepdims=True)


def swap_halves(tile):
    return pltpu.roll(tile, 64, 1)


def kernel(
    crm_in, host_in, kappa_in, counts_in, level_in, back_in, coup_in, scale_in, weight_in,
    sa, dq, host_base, back2,
    xbuf, sb, force, qsum, kron, deriv, level2, host, halo_e, halo_b,
    hbuf, kbuf, cbuf, lbuf, bbuf, coup, scale, weight,
    in_sem, arg_sem, send_sem, recv_sem,
):
    elem, band = lax.axis_index("elem"), lax.axis_index("band")
    n_elem, n_band = lax.axis_size("elem"), lax.axis_size("band")
    up_e = (lax.rem(elem + 1, n_elem), band)
    dn_e = (lax.rem(elem + n_elem - 1, n_elem), band)
    up_b = (elem, lax.rem(band + 1, n_band))
    dn_b = (elem, lax.rem(band + n_band - 1, n_band))

    small = [
        pltpu.make_async_copy(src, dst, arg_sem.at[i])
        for i, (src, dst) in enumerate((
            (host_in, hbuf), (level_in, lbuf), (scale_in, scale), (kappa_in, kbuf), (counts_in, cbuf),
            (weight_in, weight), (coup_in, coup), (back_in, bbuf),
        ))
    ]
    for copy in small:
        copy.start()
    loads = [pltpu.make_async_copy(crm_in.at[f], xbuf.at[f], in_sem.at[f]) for f in range(FIELDS)]
    for copy in loads:
        copy.start()

    barrier = pltpu.get_barrier_semaphore()
    for other in (up_e, dn_e, up_b, dn_b):
        pl.semaphore_signal(barrier, inc=1, device_id=other, device_id_type=MESH)

    def exchange(window):
        src = host.at[window]
        copies = []
        for i, (other, part, dst) in enumerate((
            (up_e, src, halo_e.at[window, 0]),
            (dn_e, src, halo_e.at[window, 1]),
            (up_b, src.at[pl.ds(COLS - 8, 8)], halo_b.at[window, 0]),
            (dn_b, src.at[pl.ds(0, 8)], halo_b.at[window, 1]),
        )):
            copies.append(pltpu.make_async_remote_copy(
                src_ref=part, dst_ref=dst,
                send_sem=send_sem.at[window, i], recv_sem=recv_sem.at[window, i],
                device_id=other, device_id_type=MESH,
            ))
        return copies

    level2[...] = jnp.zeros_like(level2)
    back2[...] = jnp.zeros_like(back2)
    src = iota((LANES, LANES), 0)
    dst = iota((LANES, LANES), 1)
    same = (src // NXC) == (dst // NXC)
    ahead = jnp.logical_and(same, (src % NXC) == (dst + 1) % NXC)
    behind = jnp.logical_and(same, (dst % NXC) == (src + 1) % NXC)
    deriv[...] = (jnp.where(behind, 0.5, 0.0) - jnp.where(ahead, 0.5, 0.0)).astype(BF16)
    zq = iota((128, LANES), 0)
    lq = iota((128, LANES), 1)
    spread_lanes = jnp.where((zq % 64) == 15 * (lq // NXC), 1.0, 0.0).astype(BF16)
    sub_row = iota((COLS, 128), 0)
    lane = iota((COLS, 128), 1)
    lane_q = iota((COLS, LANES), 1)
    low = lane < NXC

    for copy in small:
        copy.wait()

    kcol = to_column(kbuf[...])
    ccol = to_column(cbuf[...].astype(F32))
    kmid = jnp.broadcast_to(kcol, (COLS, 128))
    host[0] = jnp.where(lane == LEV, kmid, 0.0)
    host[0, :, 0:LEV] = hbuf[...]
    level2[0:NZC, :] = lbuf[...]
    level2[64 : 64 + NZC, :] = lbuf[...]
    back2[0:NZC, 0:LEV] = bbuf[...]
    row_c = iota((COLS, ROWS), 0)
    lane_r = iota((COLS, ROWS), 1)
    for f in range(FIELDS):
        value = jnp.zeros((COLS, ROWS), F32)
        for g in range(FIELDS):
            value = jnp.where(lane_r == row_c + g * COLS, coup[f, g], value)
        kron[f * COLS : (f + 1) * COLS, :] = value.astype(BF16)

    def forcing(window):
        hval = host[window]
        mapped = lax.dot_general(hval[:, 0:LEV], level2[...], NT, precision=HIGHEST, preferred_element_type=F32)
        high = mapped.astype(BF16).astype(F32)
        mhl = jnp.where(low, high, mapped - high)
        stack = jnp.concatenate([mhl] + [pltpu.roll(mhl, 128 - j, 1) for j in range(1, BLOCKS)], axis=0)
        cells = jnp.dot(stack.astype(BF16), spread_lanes, preferred_element_type=F32)
        for j in range(BLOCKS):
            for f in range(FIELDS):
                force[j, f * COLS : (f + 1) * COLS, :] = scale[f] * cells[j * COLS : (j + 1) * COLS, :]

    forcing(0)

    for f in range(FIELDS):
        loads[f].wait()
        rows = slice(f * COLS, (f + 1) * COLS)
        for j in range(BLOCKS):
            for half in range(2):
                za, zb = 30 * half + j, 30 * half + 15 + j
                ta = xbuf[f, :, (za // 2) * 128 : (za // 2 + 1) * 128]
                tb = xbuf[f, :, (zb // 2) * 128 : (zb // 2 + 1) * 128]
                if j % 2 == 0:
                    tile = jnp.where(low, ta, tb)
                else:
                    tile = swap_halves(jnp.where(low, tb, ta))
                sa[j, rows, half * 128 : (half + 1) * 128] = tile.astype(F32)

    def weighted(j):
        total = weight[0] * sa[j, 0:COLS, :]
        for f in range(1, FIELDS):
            total = total + weight[f] * sa[j, f * COLS : (f + 1) * COLS, :]
        return total

    for j in range(BLOCKS):
        qsum[j] = weighted(j)

    def shift_up(value):
        moved = pltpu.roll(value, NXC, 1)
        return jnp.where(lane_q < NXC, 0.0, moved)

    def shift_down(value):
        moved = pltpu.roll(value, LANES - NXC, 1)
        return jnp.where(lane_q >= LANES - NXC, 0.0, moved)

    cnt = jnp.broadcast_to(ccol, (COLS, LANES))

    def substep(src_ref, dst_ref, turn):
        a = jnp.where(cnt > turn.astype(F32), STEP, 0.0)
        keep = 1.0 - 2.0 * a
        for j in range(BLOCKS):
            state = src_ref[j]
            packed = state.astype(BF16)
            mix = jnp.dot(kron[...], packed, preferred_element_type=F32)
            slope = jnp.dot(packed, deriv[...], preferred_element_type=F32)
            wind = state[0:COLS]
            for f in range(FIELDS):
                rows = slice(f * COLS, (f + 1) * COLS)
                above = src_ref[j + 1, rows] if j < BLOCKS - 1 else shift_down(src_ref[0, rows])
                below = src_ref[j - 1, rows] if j > 0 else shift_up(src_ref[BLOCKS - 1, rows])
                total = (above + below) + (jnp.tanh(mix[rows]) + force[j, rows]) + wind * slope[rows]
                dst_ref[j, rows] = keep * state[rows] + a * total

    def fluxes(window, hval):
        def face(near):
            knear = jnp.broadcast_to(near[:, LEV : LEV + 1], (COLS, 128))
            return 0.5 * (kmid + knear) * (near - hval)

        prev = pltpu.roll(hval, 1, 0)
        prev = jnp.where(sub_row == 0, jnp.broadcast_to(halo_b[window, 0, 7:8, :], (COLS, 128)), prev)
        nxt = pltpu.roll(hval, COLS - 1, 0)
        nxt = jnp.where(sub_row == COLS - 1, jnp.broadcast_to(halo_b[window, 1, 0:1, :], (COLS, 128)), nxt)
        flux = face(halo_e[window, 1]) + face(halo_e[window, 0])
        return flux + face(nxt) + face(prev)

    def turns0(i, carry):
        @pl.when(i == 1)
        def _():
            pl.semaphore_wait(barrier, 4)
            for copy in exchange(0):
                copy.start()

        substep(sa, sb, 2 * i)
        substep(sb, sa, 2 * i + 1)
        return carry

    lax.fori_loop(0, SUB // 2, turns0, 0)

    for j in range(BLOCKS):
        now = weighted(j)
        dq[j] = (now - qsum[j]).astype(BF16)
        qsum[j] = now
    for copy in exchange(0):
        copy.wait()
    hval = host[0]
    tend = tendency(dq, back2)
    hnew = hval + (tend + fluxes(0, hval))
    host[1] = jnp.where(lane == LEV, kmid, hnew)
    copies = exchange(1)
    for copy in copies:
        copy.start()
    forcing(1)

    def turns1(i, carry):
        substep(sa, sb, 2 * i)
        substep(sb, sa, 2 * i + 1)
        return carry

    lax.fori_loop(0, SUB // 2, turns1, 0)

    for j in range(BLOCKS):
        dq[j] = (weighted(j) - qsum[j]).astype(BF16)
    for copy in copies:
        copy.wait()
    hval = host[1]
    host_base[0] = hval
    host_base[1] = fluxes(1, hval)


def tendency(dq, back2):
    rq = iota((LANES, 128), 0)
    cq = iota((LANES, 128), 1)
    gather_lanes = jnp.where(cq == 15 * (rq // NXC), 1.0 / NXC, 0.0).astype(BF16)
    parts = jnp.concatenate([dq[j] for j in range(BLOCKS)], axis=0)
    means = jnp.dot(parts, gather_lanes, preferred_element_type=F32)
    mixed = means[0:COLS]
    for j in range(1, BLOCKS):
        mixed = mixed + pltpu.roll(means[j * COLS : (j + 1) * COLS], j, 1)
    return jnp.dot(mixed, back2[...], precision=HIGHEST, preferred_element_type=F32)


def finish(sfin, dq, host_base, back2, crm_out, host_out, obuf, hbuf, out_sem, host_sem):
    low = iota((COLS, 128), 1) < NXC
    stores = [pltpu.make_async_copy(obuf.at[f], crm_out.at[f], out_sem.at[f]) for f in range(FIELDS)]
    for f in range(FIELDS):
        rows = slice(f * COLS, (f + 1) * COLS)
        tiles = {}
        for j in range(BLOCKS):
            for half in range(2):
                tile = sfin[j, rows, half * 128 : (half + 1) * 128].astype(BF16)
                tiles[j, half] = tile if j % 2 == 0 else swap_halves(tile)
        for t in range(TILES):
            za, zb = 2 * t, 2 * t + 1
            ta = tiles[za % 15, za // 30]
            tb = tiles[zb % 15, zb // 30]
            obuf[f, :, t * 128 : (t + 1) * 128] = jnp.where(low, ta, tb)
        stores[f].start()
    tend = tendency(dq, back2)
    hbuf[...] = (host_base[0] + (tend + host_base[1]))[:, 0:LEV]
    last = pltpu.make_async_copy(hbuf, host_out, host_sem)
    last.start()
    for copy in stores:
        copy.wait()
    last.wait()


def body(
    crm_state, host_state, kappa, substeps, coupling, level_map, field_scale, back_map, back_weight
):
    crm = jnp.transpose(crm_state[0], (1, 0, 2))
    host = jnp.transpose(host_state[:, 0, :], (1, 0))
    back = jnp.transpose(back_map, (1, 0))
    vmem = pl.BlockSpec(memory_space=pltpu.VMEM)
    hbm = pl.BlockSpec(memory_space=pltpu.HBM)
    middle = pl.pallas_call(
        kernel,
        out_shape=(
            jax.ShapeDtypeStruct((BLOCKS, ROWS, LANES), F32),
            jax.ShapeDtypeStruct((BLOCKS, COLS, LANES), BF16),
            jax.ShapeDtypeStruct((2, COLS, 128), F32),
            jax.ShapeDtypeStruct((128, 128), F32),
        ),
        in_specs=[hbm] * 9,
        out_specs=(vmem,) * 4,
        scratch_shapes=[
            pltpu.VMEM((FIELDS, COLS, CELLS), BF16),
            pltpu.VMEM((BLOCKS, ROWS, LANES), F32),
            pltpu.VMEM((BLOCKS, ROWS, LANES), F32),
            pltpu.VMEM((BLOCKS, COLS, LANES), F32),
            pltpu.VMEM((ROWS, ROWS), BF16),
            pltpu.VMEM((LANES, LANES), BF16),
            pltpu.VMEM((128, LEV), F32),
            pltpu.VMEM((WINDOWS, COLS, 128), F32),
            pltpu.VMEM((WINDOWS, 2, COLS, 128), F32),
            pltpu.VMEM((WINDOWS, 2, 8, 128), F32),
            pltpu.VMEM((COLS, LEV), F32),
            pltpu.VMEM((1, COLS), F32),
            pltpu.VMEM((1, COLS), jnp.int32),
            pltpu.VMEM((NZC, LEV), F32),
            pltpu.VMEM((NZC, LEV), F32),
            pltpu.SMEM((FIELDS, FIELDS), F32),
            pltpu.SMEM((FIELDS,), F32),
            pltpu.SMEM((FIELDS,), F32),
            pltpu.SemaphoreType.DMA((FIELDS,)),
            pltpu.SemaphoreType.DMA((8,)),
            pltpu.SemaphoreType.DMA((WINDOWS, 4)),
            pltpu.SemaphoreType.DMA((WINDOWS, 4)),
        ],
        compiler_params=pltpu.CompilerParams(
            collective_id=0, has_side_effects=True, vmem_limit_bytes=40 * 1024 * 1024
        ),
    )(*(
        pltpu.with_memory_space_constraint(x, pltpu.HBM)
        for x in (crm, host, kappa, substeps, level_map, back, coupling, field_scale, back_weight)
    ))
    crm_final, host_final = pl.pallas_call(
        finish,
        out_shape=(
            jax.ShapeDtypeStruct((FIELDS, COLS, CELLS), BF16),
            jax.ShapeDtypeStruct((COLS, LEV), F32),
        ),
        in_specs=[vmem] * 4,
        out_specs=(hbm, hbm),
        scratch_shapes=[
            pltpu.VMEM((FIELDS, COLS, CELLS), BF16),
            pltpu.VMEM((COLS, LEV), F32),
            pltpu.SemaphoreType.DMA((FIELDS,)),
            pltpu.SemaphoreType.DMA,
        ],
        compiler_params=pltpu.CompilerParams(vmem_limit_bytes=16 * 1024 * 1024),
    )(*middle)
    return (
        jnp.transpose(crm_final, (1, 0, 2))[None],
        jnp.transpose(host_final, (1, 0))[:, None, :],
    )


def solution(mesh):
    return jax.shard_map(
        body,
        mesh=mesh,
        in_specs=(
            P("elem", "band", None, None),
            P(None, "elem", "band"),
            P("elem", "band"),
            P("elem", "band"),
            P(),
            P(),
            P(),
            P(),
            P(),
        ),
        out_specs=(P("elem", "band", None, None), P(None, "elem", "band")),
        check_vma=False,
    )
```

time: 33.6 us -> 22.1 us (0.66)
  local copies, waits for them, and re-layouts: 8.71 us -> 0 us
  Pallas kernels: 23.8 us -> 21.3 us
    unnamed x19 -> x0, local copies, waits for them, and re-layouts: 8.71 us -> none
    pallas_call x1 -> x2, Pallas kernels: 23.8 us -> 21.3 us  [the longest x1 19.7 us: body(): pl.pallas_call(kernel, out_shape=(jax.ShapeDtypeStruct((BLOCKS, ROWS, LAN...]
where the time goes in v2:
time: 22.1 us; the launch traced here: 21.9 us
  Pallas kernels  21.3 us (96%)
  between operations  0.64 us (3%)
    pallas_call x1, Pallas kernels, body(): pl.pallas_call(kernel, out_shape=(jax.ShapeDtypeStruct((BLOCKS, ROWS, LAN...  19.7 us
    pallas_call x1, Pallas kernels, body(): pl.pallas_call(finish, out_shape=(jax.ShapeDtypeStruct((FIELDS, COLS, CEL...  1.58 us

profile of v2, /device:TPU:0, one launch (start us, length us, event | category | flops | bytes accessed | tf_op | source)
XLA Modules:
  0.0 21.9 jit_solution(590863971368440004)
XLA Ops:
  0.6 19.7 %shard_map.104 = (f32[15,192,256]{2,1,0:T(8,128)S(1)}, bf16[15,32,256]{2,1,0:T(8,128)(2,1)S(1)}, f32[2,32,128]{2,1,0:T(8,128)S(1)}, f32[128,128]{1,0:T(8,128)S(1)}) custom-call(bf16[6,32,3840]{2,1,0:T(8,128)(2,1)} %bitcast.13, f32[32,72]{1,0:T(8,128)} %bitcast.15, f32[1,32]{1,0:T(1,128)} %kappa_in.1, s32[1,32]{1,0:T(1,128)} %counts_in.1, f32[60,72]{1,0:T(8,128)} %level_in.1, ...), custom_call_target="tpu_custom_call" | custom-call | tf_op jit(solution)/shard_map/pallas_call | solution.py:286
  20.3 1.6 %shard_map.105 = (bf16[6,32,3840]{2,1,0:T(8,128)(2,1)}, f32[32,72]{1,0:T(8,128)}) custom-call(f32[15,192,256]{2,1,0:T(8,128)S(1)} %get-tuple-element.8.sfin, bf16[15,32,256]{2,1,0:T(8,128)(2,1)S(1)} %get-tuple-element.9.dq, f32[2,32,128]{2,1,0:T(8,128)S(1)} %get-tuple-element.10.host_base, f32[128,128]{1,0:T(8,128)S(1)} %get-tuple-element.11.back2), custom_call_target="tpu_custom_call" | custom-call | tf_op jit(solution)/shard_map/pallas_call | solution.py:327

commit v3 on v2

--- a/solution.py
+++ b/solution.py
@@ -169,18 +169,20 @@
     def substep(src_ref, dst_ref, turn):
         a = jnp.where(cnt > turn.astype(F32), STEP, 0.0)
         keep = 1.0 - 2.0 * a
-        for j in range(BLOCKS):
-            state = src_ref[j]
-            packed = state.astype(BF16)
-            mix = jnp.dot(kron[...], packed, preferred_element_type=F32)
-            slope = jnp.dot(packed, deriv[...], preferred_element_type=F32)
-            wind = state[0:COLS]
-            for f in range(FIELDS):
-                rows = slice(f * COLS, (f + 1) * COLS)
-                above = src_ref[j + 1, rows] if j < BLOCKS - 1 else shift_down(src_ref[0, rows])
-                below = src_ref[j - 1, rows] if j > 0 else shift_up(src_ref[BLOCKS - 1, rows])
-                total = (above + below) + (jnp.tanh(mix[rows]) + force[j, rows]) + wind * slope[rows]
-                dst_ref[j, rows] = keep * state[rows] + a * total
+
+        for j0 in range(0, BLOCKS, 5):
+            packed = jnp.concatenate([src_ref[j].astype(BF16) for j in range(j0, j0 + 5)], axis=0)
+            slopes = jnp.dot(packed, deriv[...], preferred_element_type=F32)
+            for j in range(j0, j0 + 5):
+                mix = jnp.dot(kron[...], packed[(j - j0) * ROWS : (j - j0 + 1) * ROWS], preferred_element_type=F32)
+                slope = slopes[(j - j0) * ROWS : (j - j0 + 1) * ROWS]
+                wind = src_ref[j, 0:COLS]
+                for f in range(FIELDS):
+                    rows = slice(f * COLS, (f + 1) * COLS)
+                    above = src_ref[j + 1, rows] if j < BLOCKS - 1 else shift_down(src_ref[0, rows])
+                    below = src_ref[j - 1, rows] if j > 0 else shift_up(src_ref[BLOCKS - 1, rows])
+                    total = (above + below) + (jnp.tanh(mix[rows]) + force[j, rows]) + wind * slope[rows]
+                    dst_ref[j, rows] = keep * src_ref[j, rows] + a * total
 
     def fluxes(window, hval):
         def face(near):
@@ -195,16 +197,13 @@
         return flux + face(nxt) + face(prev)
 
     def turns0(i, carry):
-        @pl.when(i == 1)
-        def _():
-            pl.semaphore_wait(barrier, 4)
-            for copy in exchange(0):
-                copy.start()
-
         substep(sa, sb, 2 * i)
         substep(sb, sa, 2 * i + 1)
         return carry
 
+    pl.semaphore_wait(barrier, 4)
+    for copy in exchange(0):
+        copy.start()
     lax.fori_loop(0, SUB // 2, turns0, 0)
 
     for j in range(BLOCKS):

time: 22.1 us -> 19.9 us (0.900)
  Pallas kernels: 21.3 us -> 19.1 us
    pallas_call x1, Pallas kernels: 19.7 us -> 17.5 us  [body(): pl.pallas_call(kernel, out_shape=(jax.ShapeDtypeStruct((BLOCKS, ROWS, LAN...]
where the time goes in v3:
time: 19.9 us; the launch traced here: 19.7 us
  Pallas kernels  19.1 us (96%)
  between operations  0.64 us (3%)
    pallas_call x1, Pallas kernels, body(): pl.pallas_call(kernel, out_shape=(jax.ShapeDtypeStruct((BLOCKS, ROWS, LAN...  17.5 us
    pallas_call x1, Pallas kernels, body(): pl.pallas_call(finish, out_shape=(jax.ShapeDtypeStruct((FIELDS, COLS, CEL...  1.58 us

profile of v3, /device:TPU:0, one launch (start us, length us, event | category | flops | bytes accessed | tf_op | source)
XLA Modules:
  0.0 19.7 jit_solution(16945772889154752078)
XLA Ops:
  0.6 17.5 %shard_map.104 = (f32[15,192,256]{2,1,0:T(8,128)S(1)}, bf16[15,32,256]{2,1,0:T(8,128)(2,1)S(1)}, f32[2,32,128]{2,1,0:T(8,128)S(1)}, f32[128,128]{1,0:T(8,128)S(1)}) custom-call(bf16[6,32,3840]{2,1,0:T(8,128)(2,1)} %bitcast.13, f32[32,72]{1,0:T(8,128)} %bitcast.15, f32[1,32]{1,0:T(1,128)} %kappa_in.1, s32[1,32]{1,0:T(1,128)} %counts_in.1, f32[60,72]{1,0:T(8,128)} %level_in.1, ...), custom_call_target="tpu_custom_call" | custom-call | tf_op jit(solution)/shard_map/pallas_call | solution.py:285
  18.1 1.6 %shard_map.105 = (bf16[6,32,3840]{2,1,0:T(8,128)(2,1)}, f32[32,72]{1,0:T(8,128)}) custom-call(f32[15,192,256]{2,1,0:T(8,128)S(1)} %get-tuple-element.8.sfin, bf16[15,32,256]{2,1,0:T(8,128)(2,1)S(1)} %get-tuple-element.9.dq, f32[2,32,128]{2,1,0:T(8,128)S(1)} %get-tuple-element.10.host_base, f32[128,128]{1,0:T(8,128)S(1)} %get-tuple-element.11.back2), custom_call_target="tpu_custom_call" | custom-call | tf_op jit(solution)/shard_map/pallas_call | solution.py:326

commit v4 on v3

--- a/solution.py
+++ b/solution.py
@@ -21,7 +21,6 @@
 MESH = pl.DeviceIdType.MESH
 F32 = jnp.float32
 BF16 = jnp.bfloat16
-HIGHEST = lax.Precision.HIGHEST
 NT = (((1,), (1,)), ((), ()))
 
 
@@ -40,8 +39,8 @@
 
 def kernel(
     crm_in, host_in, kappa_in, counts_in, level_in, back_in, coup_in, scale_in, weight_in,
-    sa, dq, host_base, back2,
-    xbuf, sb, force, qsum, kron, deriv, level2, host, halo_e, halo_b,
+    obuf, host_fin,
+    xbuf, sa, sb, dq, back2, force, qsum, kron, deriv, level2, square, host, halo_e, halo_b,
     hbuf, kbuf, cbuf, lbuf, bbuf, coup, scale, weight,
     in_sem, arg_sem, send_sem, recv_sem,
 ):
@@ -85,8 +84,12 @@
             ))
         return copies
 
-    level2[...] = jnp.zeros_like(level2)
-    back2[...] = jnp.zeros_like(back2)
+    def send_borders():
+        pl.semaphore_wait(barrier, 4)
+        for copy in exchange(0):
+            copy.start()
+
+    pad_l = jnp.zeros((128, 128), F32)
     src = iota((LANES, LANES), 0)
     dst = iota((LANES, LANES), 1)
     same = (src // NXC) == (dst // NXC)
@@ -109,9 +112,22 @@
     kmid = jnp.broadcast_to(kcol, (COLS, 128))
     host[0] = jnp.where(lane == LEV, kmid, 0.0)
     host[0, :, 0:LEV] = hbuf[...]
-    level2[0:NZC, :] = lbuf[...]
-    level2[64 : 64 + NZC, :] = lbuf[...]
-    back2[0:NZC, 0:LEV] = bbuf[...]
+    square[...] = pad_l
+    square[0:NZC, 0:LEV] = lbuf[...]
+    square[64 : 64 + NZC, 0:LEV] = lbuf[...]
+    whole = square[...]
+    high = whole.astype(BF16)
+    rest = (whole - high.astype(F32)).astype(BF16)
+    level2[:, 0:128] = high
+    level2[:, 128:256] = high
+    level2[:, 256:384] = rest
+    square[...] = pad_l
+    square[0:NZC, 0:LEV] = bbuf[...]
+    square[64 : 64 + NZC, 0:LEV] = bbuf[...]
+    whole = square[...]
+    high = whole.astype(BF16)
+    back2[0:128, :] = high
+    back2[128:256, :] = (whole - high.astype(F32)).astype(BF16)
     row_c = iota((COLS, ROWS), 0)
     lane_r = iota((COLS, ROWS), 1)
     for f in range(FIELDS):
@@ -122,7 +138,11 @@
 
     def forcing(window):
         hval = host[window]
-        mapped = lax.dot_general(hval[:, 0:LEV], level2[...], NT, precision=HIGHEST, preferred_element_type=F32)
+        hval = jnp.where(lane < LEV, hval, 0.0)
+        hhigh = hval.astype(BF16)
+        hlow = (hval - hhigh.astype(F32)).astype(BF16)
+        triple = jnp.concatenate([hhigh, hlow, hhigh], axis=1)
+        mapped = lax.dot_general(triple, level2[...], NT, preferred_element_type=F32)
         high = mapped.astype(BF16).astype(F32)
         mhl = jnp.where(low, high, mapped - high)
         stack = jnp.concatenate([mhl] + [pltpu.roll(mhl, 128 - j, 1) for j in range(1, BLOCKS)], axis=0)
@@ -132,6 +152,10 @@
                 force[j, f * COLS : (f + 1) * COLS, :] = scale[f] * cells[j * COLS : (j + 1) * COLS, :]
 
     forcing(0)
+
+    @pl.when(elem != 0)
+    def _():
+        send_borders()
 
     for f in range(FIELDS):
         loads[f].wait()
@@ -198,12 +222,13 @@
 
     def turns0(i, carry):
         substep(sa, sb, 2 * i)
+        @pl.when(jnp.logical_and(elem == 0, i == 0))
+        def _():
+            send_borders()
+
         substep(sb, sa, 2 * i + 1)
         return carry
 
-    pl.semaphore_wait(barrier, 4)
-    for copy in exchange(0):
-        copy.start()
     lax.fori_loop(0, SUB // 2, turns0, 0)
 
     for j in range(BLOCKS):
@@ -230,11 +255,23 @@
 
     for j in range(BLOCKS):
         dq[j] = (weighted(j) - qsum[j]).astype(BF16)
+    tend = tendency(dq, back2)
+    for f in range(FIELDS):
+        rows = slice(f * COLS, (f + 1) * COLS)
+        tiles = {}
+        for j in range(BLOCKS):
+            for half in range(2):
+                tile = sa[j, rows, half * 128 : (half + 1) * 128].astype(BF16)
+                tiles[j, half] = tile if j % 2 == 0 else swap_halves(tile)
+        for t in range(TILES):
+            za, zb = 2 * t, 2 * t + 1
+            ta = tiles[za % 15, za // 30]
+            tb = tiles[zb % 15, zb // 30]
+            obuf[f, :, t * 128 : (t + 1) * 128] = jnp.where(low, ta, tb)
     for copy in copies:
         copy.wait()
     hval = host[1]
-    host_base[0] = hval
-    host_base[1] = fluxes(1, hval)
+    host_fin[...] = (hval + (tend + fluxes(1, hval)))[:, 0:LEV]
 
 
 def tendency(dq, back2):
@@ -246,32 +283,19 @@
     mixed = means[0:COLS]
     for j in range(1, BLOCKS):
         mixed = mixed + pltpu.roll(means[j * COLS : (j + 1) * COLS], j, 1)
-    return jnp.dot(mixed, back2[...], precision=HIGHEST, preferred_element_type=F32)
-
-
-def finish(sfin, dq, host_base, back2, crm_out, host_out, obuf, hbuf, out_sem, host_sem):
-    low = iota((COLS, 128), 1) < NXC
-    stores = [pltpu.make_async_copy(obuf.at[f], crm_out.at[f], out_sem.at[f]) for f in range(FIELDS)]
-    for f in range(FIELDS):
-        rows = slice(f * COLS, (f + 1) * COLS)
-        tiles = {}
-        for j in range(BLOCKS):
-            for half in range(2):
-                tile = sfin[j, rows, half * 128 : (half + 1) * 128].astype(BF16)
-                tiles[j, half] = tile if j % 2 == 0 else swap_halves(tile)
-        for t in range(TILES):
-            za, zb = 2 * t, 2 * t + 1
-            ta = tiles[za % 15, za // 30]
-            tb = tiles[zb % 15, zb // 30]
-            obuf[f, :, t * 128 : (t + 1) * 128] = jnp.where(low, ta, tb)
-        stores[f].start()
-    tend = tendency(dq, back2)
-    hbuf[...] = (host_base[0] + (tend + host_base[1]))[:, 0:LEV]
-    last = pltpu.make_async_copy(hbuf, host_out, host_sem)
-    last.start()
+    high = mixed.astype(BF16)
+    both = high.astype(F32) + pltpu.roll(mixed - high.astype(F32), 64, 1)
+    pair = jnp.concatenate([both.astype(BF16), high], axis=1)
+    return jnp.dot(pair, back2[...], preferred_element_type=F32)
+
+
+def finish(crm, host, crm_out, host_out, out_sem, host_sem):
+    stores = [pltpu.make_async_copy(crm.at[f], crm_out.at[f], out_sem.at[f]) for f in range(FIELDS)]
+    stores.append(pltpu.make_async_copy(host, host_out, host_sem))
+    for copy in stores:
+        copy.start()
     for copy in stores:
         copy.wait()
-    last.wait()
 
 
 def body(
@@ -285,21 +309,23 @@
     middle = pl.pallas_call(
         kernel,
         out_shape=(
-            jax.ShapeDtypeStruct((BLOCKS, ROWS, LANES), F32),
-            jax.ShapeDtypeStruct((BLOCKS, COLS, LANES), BF16),
-            jax.ShapeDtypeStruct((2, COLS, 128), F32),
-            jax.ShapeDtypeStruct((128, 128), F32),
+            jax.ShapeDtypeStruct((FIELDS, COLS, CELLS), BF16),
+            jax.ShapeDtypeStruct((COLS, LEV), F32),
         ),
         in_specs=[hbm] * 9,
-        out_specs=(vmem,) * 4,
+        out_specs=(vmem,) * 2,
         scratch_shapes=[
             pltpu.VMEM((FIELDS, COLS, CELLS), BF16),
             pltpu.VMEM((BLOCKS, ROWS, LANES), F32),
             pltpu.VMEM((BLOCKS, ROWS, LANES), F32),
+            pltpu.VMEM((BLOCKS, COLS, LANES), BF16),
+            pltpu.VMEM((256, 128), BF16),
+            pltpu.VMEM((BLOCKS, ROWS, LANES), F32),
             pltpu.VMEM((BLOCKS, COLS, LANES), F32),
             pltpu.VMEM((ROWS, ROWS), BF16),
             pltpu.VMEM((LANES, LANES), BF16),
-            pltpu.VMEM((128, LEV), F32),
+            pltpu.VMEM((128, 3 * 128), BF16),
+            pltpu.VMEM((128, 128), F32),
             pltpu.VMEM((WINDOWS, COLS, 128), F32),
             pltpu.VMEM((WINDOWS, 2, COLS, 128), F32),
             pltpu.VMEM((WINDOWS, 2, 8, 128), F32),
@@ -329,11 +355,9 @@
             jax.ShapeDtypeStruct((FIELDS, COLS, CELLS), BF16),
             jax.ShapeDtypeStruct((COLS, LEV), F32),
         ),
-        in_specs=[vmem] * 4,
+        in_specs=[vmem] * 2,
         out_specs=(hbm, hbm),
         scratch_shapes=[
-            pltpu.VMEM((FIELDS, COLS, CELLS), BF16),
-            pltpu.VMEM((COLS, LEV), F32),
             pltpu.SemaphoreType.DMA((FIELDS,)),
             pltpu.SemaphoreType.DMA,
         ],

time: 19.9 us -> 19.4 us (0.975)
  Pallas kernels: 19.1 us -> 18.6 us
    pallas_call x1, Pallas kernels: 1.58 us -> 1.16 us  [body(): pl.pallas_call(finish, out_shape=(jax.ShapeDtypeStruct((FIELDS, COLS, CEL...]
where the time goes in v4:
time: 19.4 us; the launch traced here: 19.2 us
  Pallas kernels  18.6 us (96%)
  between operations  0.64 us (3%)
    pallas_call x1, Pallas kernels, body(): pl.pallas_call(kernel, out_shape=(jax.ShapeDtypeStruct((FIELDS, COLS, CEL...  17.4 us
    pallas_call x1, Pallas kernels, body(): pl.pallas_call(finish, out_shape=(jax.ShapeDtypeStruct((FIELDS, COLS, CEL...  1.16 us

profile of v4, /device:TPU:0, one launch (start us, length us, event | category | flops | bytes accessed | tf_op | source)
XLA Modules:
  0.0 19.2 jit_solution(13681526955594990967)
XLA Ops:
  0.6 17.4 %shard_map.104 = (bf16[6,32,3840]{2,1,0:T(8,128)(2,1)S(1)}, f32[32,72]{1,0:T(8,128)S(1)}) custom-call(bf16[6,32,3840]{2,1,0:T(8,128)(2,1)} %bitcast.13, f32[32,72]{1,0:T(8,128)} %bitcast.15, f32[1,32]{1,0:T(1,128)} %kappa_in.1, s32[1,32]{1,0:T(1,128)} %counts_in.1, f32[60,72]{1,0:T(8,128)} %level_in.1, f32[60,72]{1,0:T(8,128)} %bitcast.14, f32[6,6]{1,0:T(8,128)} %coup_in.1, ...), custom_call_target="tpu_custom_call" | custom-call | tf_op jit(solution)/shard_map/pallas_call | solution.py:309
  18.1 1.2 %shard_map.105 = (bf16[6,32,3840]{2,1,0:T(8,128)(2,1)}, f32[32,72]{1,0:T(8,128)}) custom-call(bf16[6,32,3840]{2,1,0:T(8,128)(2,1)S(1)} %get-tuple-element.6.crm, f32[32,72]{1,0:T(8,128)S(1)} %get-tuple-element.7.host), custom_call_target="tpu_custom_call" | custom-call | tf_op jit(solution)/shard_map/pallas_call | solution.py:352

commit v5 on v4

--- a/solution.py
+++ b/solution.py
@@ -235,10 +235,11 @@
         now = weighted(j)
         dq[j] = (now - qsum[j]).astype(BF16)
         qsum[j] = now
-    for copy in exchange(0):
-        copy.wait()
+    tend = tendency(dq, back2)
     hval = host[0]
-    tend = tendency(dq, back2)
+    first = exchange(0)
+    for copy in first:
+        copy.wait_recv()
     hnew = hval + (tend + fluxes(0, hval))
     host[1] = jnp.where(lane == LEV, kmid, hnew)
     copies = exchange(1)
@@ -268,6 +269,8 @@
             ta = tiles[za % 15, za // 30]
             tb = tiles[zb % 15, zb // 30]
             obuf[f, :, t * 128 : (t + 1) * 128] = jnp.where(low, ta, tb)
+    for copy in first:
+        copy.wait_send()
     for copy in copies:
         copy.wait()
     hval = host[1]

time: 19.4 us -> 19 us (0.979)
  Pallas kernels: 18.6 us -> 18.2 us
    pallas_call x1, Pallas kernels: 17.4 us -> 17 us  [body(): pl.pallas_call(kernel, out_shape=(jax.ShapeDtypeStruct((FIELDS, COLS, CEL...]
where the time goes in v5:
time: 19 us; the launch traced here: 18.8 us
  Pallas kernels  18.2 us (96%)
  between operations  0.64 us (3%)
    pallas_call x1, Pallas kernels, body(): pl.pallas_call(kernel, out_shape=(jax.ShapeDtypeStruct((FIELDS, COLS, CEL...  17 us
    pallas_call x1, Pallas kernels, body(): pl.pallas_call(finish, out_shape=(jax.ShapeDtypeStruct((FIELDS, COLS, CEL...  1.16 us

profile of v5, /device:TPU:0, one launch (start us, length us, event | category | flops | bytes accessed | tf_op | source)
XLA Modules:
  0.0 18.8 jit_solution(18396194311053044001)
XLA Ops:
  0.6 17.0 %shard_map.104 = (bf16[6,32,3840]{2,1,0:T(8,128)(2,1)S(1)}, f32[32,72]{1,0:T(8,128)S(1)}) custom-call(bf16[6,32,3840]{2,1,0:T(8,128)(2,1)} %bitcast.13, f32[32,72]{1,0:T(8,128)} %bitcast.15, f32[1,32]{1,0:T(1,128)} %kappa_in.1, s32[1,32]{1,0:T(1,128)} %counts_in.1, f32[60,72]{1,0:T(8,128)} %level_in.1, f32[60,72]{1,0:T(8,128)} %bitcast.14, f32[6,6]{1,0:T(8,128)} %coup_in.1, ...), custom_call_target="tpu_custom_call" | custom-call | tf_op jit(solution)/shard_map/pallas_call | solution.py:312
  17.6 1.2 %shard_map.105 = (bf16[6,32,3840]{2,1,0:T(8,128)(2,1)}, f32[32,72]{1,0:T(8,128)}) custom-call(bf16[6,32,3840]{2,1,0:T(8,128)(2,1)S(1)} %get-tuple-element.6.crm, f32[32,72]{1,0:T(8,128)S(1)} %get-tuple-element.7.host), custom_call_target="tpu_custom_call" | custom-call | tf_op jit(solution)/shard_map/pallas_call | solution.py:355
